TPU v7x, 256 devices: a whole 4x4x8 slice. The times are simulated.
256 devices in a mesh: env: 4 (over x), wave: 64 (over y, z, core).
Axes of the slice: x: 4, y: 4, z: 8, core: 2. Of those that a mesh axis runs over, the one named last changes fastest.
Arguments:
- psi: bfloat16 [4096, 128, 128], P('wave'), may hold values from -6 to 6
- left_env: bfloat16 [40, 64, 128, 128], P('env', 'wave'), may hold values from -0.5 to 0.5
- right_env: bfloat16 [40, 64, 128, 128], P('env', 'wave'), may hold values from -0.078125 to 0.078125
- left_sector: int32 [4096, 1], P('wave'), may hold values from 0 to 63; in each aligned block of 64 rows (0 to 63, 64 to 127, ...) at most 2 rows name the same one
- right_sector: int32 [4096, 1], P('wave'), may hold values from 0 to 63
- sector_owner: int32 [64], replicated, may hold values from 0 to 63, each once
- sector_rows: int32 [64], replicated, may hold values from 64 to 128
Outputs:
- h_psi: bfloat16 [4096, 128, 128], P('wave', 'env')
Inputs may be any that keep to these rules, and one draw needn't show every extreme that they name: `left_sector`: among the 64 blocks of one wave index no left sector appears more than 2 times, and some sector appears exactly 2 times. `sector_owner`: each wave index holds the environments of exactly one sector.
All inputs are finite; a program needn't handle non-finite values.
Results may differ from a plain program's by a relative error of at most 0.013.
Values may be sent and summed in bfloat16 or wider, within the bound.
A program may use at most 128 MiB of HBM per device.

v0:
```python
import jax
import jax.numpy as jnp
from jax import lax
from jax.sharding import PartitionSpec as P


def on_device(psi, left_env, right_env, left_sector, right_sector, sector_owner, sector_rows):
    nwave = lax.axis_size("wave")
    nenv = lax.axis_size("env")
    count = psi.shape[0]
    width = psi.shape[1]
    capacity = max(2, 2 * count // nwave)
    sectors = sector_owner.shape[0]
    labels = jnp.arange(sectors, dtype=jnp.int32)
    lsec = left_sector[:, 0]
    rsec = right_sector[:, 0]
    lhot = (lsec[:, None] == labels[None, :]).astype(jnp.int32)
    rhot = (rsec[:, None] == labels[None, :]).astype(jnp.int32)
    target = jnp.sum(lhot * sector_owner[None, :], axis=1)
    rplace = jnp.sum(rhot * sector_owner[None, :], axis=1)
    lrows = jnp.sum(lhot * sector_rows[None, :], axis=1)
    rrows = jnp.sum(rhot * sector_rows[None, :], axis=1)
    line = jnp.arange(width, dtype=jnp.int32)
    full_mask = (line[None, :, None] < lrows[:, None, None]) & (
        line[None, None, :] < rrows[:, None, None]
    )
    masked = jnp.where(full_mask, psi, jnp.zeros_like(psi))
    peers = jnp.arange(nwave, dtype=jnp.int32)
    dest_hot = (target[:, None] == peers[None, :]).astype(jnp.int32)
    rank = jnp.sum((jnp.cumsum(dest_hot, axis=0) - dest_hot) * dest_hot, axis=1)
    slot = target * capacity + rank
    outgoing = jnp.zeros((nwave * capacity, width, width), jnp.bfloat16).at[slot].set(masked)
    outgoing = outgoing.reshape(nwave, capacity, width, width)
    places = jnp.zeros((nwave * capacity,), jnp.int32).at[slot].set(rplace)
    places = places.reshape(nwave, capacity, 1)
    left_own = left_env[:, 0]
    right_all = lax.all_gather(right_env, "wave", axis=1, tiled=True)

    def slot_work(items):
        blocks, where = items
        inner = jnp.einsum("wab,nbc->nwac", left_own, blocks, preferred_element_type=jnp.float32)
        inner = inner.astype(jnp.bfloat16)
        chosen = jnp.take(right_all, where, axis=1)
        part = jnp.einsum("nwac,wncd->nad", inner, chosen, preferred_element_type=jnp.float32)
        return part.astype(jnp.bfloat16)

    blocks = lax.all_to_all(outgoing, "wave", split_axis=0, concat_axis=0, tiled=True)
    where = lax.all_to_all(places, "wave", split_axis=0, concat_axis=0, tiled=True)
    sources = blocks.shape[0]
    items = blocks.shape[1]
    groups = sources // 8
    flat_blocks = blocks.reshape(groups, 8 * items, width, width)
    flat_where = where.reshape(groups, 8 * items)
    parts = lax.map(slot_work, (flat_blocks, flat_where))
    parts = parts.reshape(sources, items, width, width)
    returned = lax.all_to_all(parts, "wave", split_axis=0, concat_axis=0, tiled=True)
    rows_here = returned.shape[2]
    home = returned.reshape(nwave * capacity, rows_here, width)[slot]
    total = lax.psum_scatter(
        home.astype(jnp.float32).astype(jnp.bfloat16), "env", scatter_dimension=1, tiled=True
    ).astype(jnp.float32)
    share = width // nenv
    base = lax.axis_index("env") * share
    row_line = base + jnp.arange(share, dtype=jnp.int32)
    out_mask = (row_line[None, :, None] < lrows[:, None, None]) & (
        line[None, None, :] < rrows[:, None, None]
    )
    return jnp.where(out_mask, total, jnp.zeros_like(total)).astype(jnp.bfloat16)


def solution(mesh):
    return jax.shard_map(
        on_device,
        mesh=mesh,
        in_specs=(
            P("wave", None, None),
            P("env", "wave", None, None),
            P("env", "wave", None, None),
            P("wave", None),
            P("wave", None),
            P(),
            P(),
        ),
        out_specs=P("wave", "env", None),
        check_vma=False,
    )
```

profile of v0, /device:TPU:1, one launch (start us, length us, event | category | flops | bytes accessed | tf_op | source)
XLA Modules:
  0.0 476.5 jit_solution(2104947256432421240)
XLA Ops:
  10.1 13.2 %all-to-all-start.1 = ((s32[64,2,1]{1,2,0:T(1,128)}), s32[64,2,1]{1,2,0:T(1,128)S(1)}, u32[]{:S(2)}, u32[]{:S(2)}) async-start(s32[64,2,1]{1,2,0:T(1,128)} %bitcast.19), calls=%async_computation.1 | async-start | bytes 65536 | tf_op jit(solution)/shard_map/all_to_all | solution.py:48
  29.6 8.6 %scatter_fusion = bf16[128,128,128]{2,1,0:T(8,128)(2,1)} fusion(bf16[128,128,128]{2,1,0:T(8,128)(2,1)} %broadcast_in_dim.21, s32[64]{0:T(128)S(1)} %fusion.40, bf16[64,128,128]{2,1,0:T(8,128)(2,1)S(1)} %and_select_fusion), kind=kCustom, calls=%fused_computation.2 | custom fusion | bytes 6291712 | tf_op jit(solution)/shard_map/scatter | solution.py:32
  38.2 10.5 %all-to-all-start = ((bf16[64,2,128,128]{3,2,1,0:T(8,128)(2,1)}), bf16[64,2,128,128]{3,2,1,0:T(8,128)(2,1)}, u32[]{:S(2)}, u32[]{:S(2)}) async-start(bf16[64,2,128,128]{3,2,1,0:T(8,128)(2,1)} %bitcast.83), calls=%async_computation | async-start | bytes 8388608 | tf_op jit(solution)/shard_map/all_to_all | solution.py:47
  50.1 130.4 %all-to-all-done = bf16[64,2,128,128]{3,2,1,0:T(8,128)(2,1)} async-done(((bf16[64,2,128,128]{3,2,1,0:T(8,128)(2,1)}), bf16[64,2,128,128]{3,2,1,0:T(8,128)(2,1)}, u32[]{:S(2)}, u32[]{:S(2)}) %all-to-all-start) | async-done | bytes 4194336 | tf_op jit(solution)/shard_map/all_to_all | solution.py:47
  180.4 6.5 %copy.9 = bf16[64,2,128,128]{2,3,1,0:T(8,128)(2,1)} copy(bf16[64,2,128,128]{3,2,1,0:T(8,128)(2,1)} %all-to-all-done) | data formatting | bytes 8388608 | tf_op jit(solution)/shard_map/all_to_all | solution.py:47
  186.9 8.1 %all-gather.2.cloned.1.call-done = bf16[10,64,128,128]{3,2,1,0:T(8,128)(2,1)} async-done(((bf16[10,1,128,128]{3,2,1,0:T(8,128)(2,1)}), bf16[10,64,128,128]{3,2,1,0:T(8,128)(2,1)}) %all-gather.2.cloned.1.call-update) | async-done | bytes 20971536 | tf_op jit(solution)/shard_map/all_gather | solution.py:37
  195.1 135.8 %while.10 = (s32[]{:T(128)}, bf16[8,16,128,128]{3,2,1,0:T(8,128)(2,1)}, bf16[8,16,128,128]{2,3,1,0:T(8,128)(2,1)}, bf16[10,128,128]{2,1,0:T(8,128)(2,1)S(1)}, s3...) while((s32[]{:T(128)}, bf16[8,16,128,128]{3,2,1,0:T(8,128)(2,1)}, ...), condition=%wide.region_9.10_spmd, body=%wide.region_8.9_spmd.sunk | while | flops 1347683456 | bytes 17110452 | solution.py:54
  195.1 10.5 %gather_fusion = bf16[16,10,128,128]{3,2,1,0:T(8,128)(2,1)} fusion(bf16[10,64,128,128]{3,2,1,0:T(8,128)(2,1)} %get-tuple-element.112, s32[1024]{0:T(1024)S(1)} %pad_clamp_fusion.3), kind=kCustom, calls=%fused_computation.clone.1 | custom fusion | bytes 10485824 | tf_op jit(solution)/shard_map/while/body/eval_jaxpr/jit(_take)/gather | solution.py:43
  212.0 10.5 %gather_fusion = bf16[16,10,128,128]{3,2,1,0:T(8,128)(2,1)} fusion(bf16[10,64,128,128]{3,2,1,0:T(8,128)(2,1)} %get-tuple-element.112, s32[1024]{0:T(1024)S(1)} %pad_clamp_fusion.3), kind=kCustom, calls=%fused_computation.clone.1 | custom fusion | bytes 10485824 | tf_op jit(solution)/shard_map/while/body/eval_jaxpr/jit(_take)/gather | solution.py:43
  222.6 6.4 %fusion.54 = bf16[8,16,128,128]{3,2,1,0:T(8,128)(2,1)} fusion(bf16[8,16,128,128]{3,2,1,0:T(8,128)(2,1)} %get-tuple-element.101, s32[]{:T(128)} %get-tuple-element.100, bf16[16,10,128,128]{3,2,1,0:T(8,128)(2,1)} %gather_fusion, pred[16]{0:T(512)(128)(4,1)S(1)} %compare_and_fusion.2, bf16[8,16,128,128]{2,3,1,0:T(8,128)(2,1)} %get-tuple-element.109, ...), kind=kOutput, calls=%fused_computation.15.clone.1 | convolution fusion | flops 1347682304 | bytes 6620176 | tf_op jit(solution)/shard_map/while/body/eval_jaxpr/nwac,wncd->nad/dot_general | solution.py:44
  229.0 10.5 %gather_fusion = bf16[16,10,128,128]{3,2,1,0:T(8,128)(2,1)} fusion(bf16[10,64,128,128]{3,2,1,0:T(8,128)(2,1)} %get-tuple-element.112, s32[1024]{0:T(1024)S(1)} %pad_clamp_fusion.3), kind=kCustom, calls=%fused_computation.clone.1 | custom fusion | bytes 10485824 | tf_op jit(solution)/shard_map/while/body/eval_jaxpr/jit(_take)/gather | solution.py:43
  239.5 6.4 %fusion.54 = bf16[8,16,128,128]{3,2,1,0:T(8,128)(2,1)} fusion(bf16[8,16,128,128]{3,2,1,0:T(8,128)(2,1)} %get-tuple-element.101, s32[]{:T(128)} %get-tuple-element.100, bf16[16,10,128,128]{3,2,1,0:T(8,128)(2,1)} %gather_fusion, pred[16]{0:T(512)(128)(4,1)S(1)} %compare_and_fusion.2, bf16[8,16,128,128]{2,3,1,0:T(8,128)(2,1)} %get-tuple-element.109, ...), kind=kOutput, calls=%fused_computation.15.clone.1 | convolution fusion | flops 1347682304 | bytes 6620176 | tf_op jit(solution)/shard_map/while/body/eval_jaxpr/nwac,wncd->nad/dot_general | solution.py:44
  246.0 10.5 %gather_fusion = bf16[16,10,128,128]{3,2,1,0:T(8,128)(2,1)} fusion(bf16[10,64,128,128]{3,2,1,0:T(8,128)(2,1)} %get-tuple-element.112, s32[1024]{0:T(1024)S(1)} %pad_clamp_fusion.3), kind=kCustom, calls=%fused_computation.clone.1 | custom fusion | bytes 10485824 | tf_op jit(solution)/shard_map/while/body/eval_jaxpr/jit(_take)/gather | solution.py:43
  256.5 6.4 %fusion.54 = bf16[8,16,128,128]{3,2,1,0:T(8,128)(2,1)} fusion(bf16[8,16,128,128]{3,2,1,0:T(8,128)(2,1)} %get-tuple-element.101, s32[]{:T(128)} %get-tuple-element.100, bf16[16,10,128,128]{3,2,1,0:T(8,128)(2,1)} %gather_fusion, pred[16]{0:T(512)(128)(4,1)S(1)} %compare_and_fusion.2, bf16[8,16,128,128]{2,3,1,0:T(8,128)(2,1)} %get-tuple-element.109, ...), kind=kOutput, calls=%fused_computation.15.clone.1 | convolution fusion | flops 1347682304 | bytes 6620176 | tf_op jit(solution)/shard_map/while/body/eval_jaxpr/nwac,wncd->nad/dot_general | solution.py:44
  263.0 10.5 %gather_fusion = bf16[16,10,128,128]{3,2,1,0:T(8,128)(2,1)} fusion(bf16[10,64,128,128]{3,2,1,0:T(8,128)(2,1)} %get-tuple-element.112, s32[1024]{0:T(1024)S(1)} %pad_clamp_fusion.3), kind=kCustom, calls=%fused_computation.clone.1 | custom fusion | bytes 10485824 | tf_op jit(solution)/shard_map/while/body/eval_jaxpr/jit(_take)/gather | solution.py:43
  279.9 10.5 %gather_fusion = bf16[16,10,128,128]{3,2,1,0:T(8,128)(2,1)} fusion(bf16[10,64,128,128]{3,2,1,0:T(8,128)(2,1)} %get-tuple-element.112, s32[1024]{0:T(1024)S(1)} %pad_clamp_fusion.3), kind=kCustom, calls=%fused_computation.clone.1 | custom fusion | bytes 10485824 | tf_op jit(solution)/shard_map/while/body/eval_jaxpr/jit(_take)/gather | solution.py:43
  290.5 6.4 %fusion.54 = bf16[8,16,128,128]{3,2,1,0:T(8,128)(2,1)} fusion(bf16[8,16,128,128]{3,2,1,0:T(8,128)(2,1)} %get-tuple-element.101, s32[]{:T(128)} %get-tuple-element.100, bf16[16,10,128,128]{3,2,1,0:T(8,128)(2,1)} %gather_fusion, pred[16]{0:T(512)(128)(4,1)S(1)} %compare_and_fusion.2, bf16[8,16,128,128]{2,3,1,0:T(8,128)(2,1)} %get-tuple-element.109, ...), kind=kOutput, calls=%fused_computation.15.clone.1 | convolution fusion | flops 1347682304 | bytes 6620176 | tf_op jit(solution)/shard_map/while/body/eval_jaxpr/nwac,wncd->nad/dot_general | solution.py:44
  296.9 10.5 %gather_fusion = bf16[16,10,128,128]{3,2,1,0:T(8,128)(2,1)} fusion(bf16[10,64,128,128]{3,2,1,0:T(8,128)(2,1)} %get-tuple-element.112, s32[1024]{0:T(1024)S(1)} %pad_clamp_fusion.3), kind=kCustom, calls=%fused_computation.clone.1 | custom fusion | bytes 10485824 | tf_op jit(solution)/shard_map/while/body/eval_jaxpr/jit(_take)/gather | solution.py:43
  307.4 6.4 %fusion.54 = bf16[8,16,128,128]{3,2,1,0:T(8,128)(2,1)} fusion(bf16[8,16,128,128]{3,2,1,0:T(8,128)(2,1)} %get-tuple-element.101, s32[]{:T(128)} %get-tuple-element.100, bf16[16,10,128,128]{3,2,1,0:T(8,128)(2,1)} %gather_fusion, pred[16]{0:T(512)(128)(4,1)S(1)} %compare_and_fusion.2, bf16[8,16,128,128]{2,3,1,0:T(8,128)(2,1)} %get-tuple-element.109, ...), kind=kOutput, calls=%fused_computation.15.clone.1 | convolution fusion | flops 1347682304 | bytes 6620176 | tf_op jit(solution)/shard_map/while/body/eval_jaxpr/nwac,wncd->nad/dot_general | solution.py:44
  313.9 10.5 %gather_fusion = bf16[16,10,128,128]{3,2,1,0:T(8,128)(2,1)} fusion(bf16[10,64,128,128]{3,2,1,0:T(8,128)(2,1)} %get-tuple-element.112, s32[1024]{0:T(1024)S(1)} %pad_clamp_fusion.3), kind=kCustom, calls=%fused_computation.clone.1 | custom fusion | bytes 10485824 | tf_op jit(solution)/shard_map/while/body/eval_jaxpr/jit(_take)/gather | solution.py:43
  324.4 6.4 %fusion.54 = bf16[8,16,128,128]{3,2,1,0:T(8,128)(2,1)} fusion(bf16[8,16,128,128]{3,2,1,0:T(8,128)(2,1)} %get-tuple-element.101, s32[]{:T(128)} %get-tuple-element.100, bf16[16,10,128,128]{3,2,1,0:T(8,128)(2,1)} %gather_fusion, pred[16]{0:T(512)(128)(4,1)S(1)} %compare_and_fusion.2, bf16[8,16,128,128]{2,3,1,0:T(8,128)(2,1)} %get-tuple-element.109, ...), kind=kOutput, calls=%fused_computation.15.clone.1 | convolution fusion | flops 1347682304 | bytes 6620176 | tf_op jit(solution)/shard_map/while/body/eval_jaxpr/nwac,wncd->nad/dot_general | solution.py:44
  330.8 7.6 %all-to-all-start.2 = ((bf16[64,2,128,128]{3,2,1,0:T(8,128)(2,1)}), bf16[64,2,128,128]{3,2,1,0:T(8,128)(2,1)}, u32[]{:S(2)}, u32[]{:S(2)}) async-start(bf16[64,2,128,128]{3,2,1,0:T(8,128)(2,1)} %bitcast.85), calls=%async_computation.2 | async-start | bytes 8388608 | tf_op jit(solution)/shard_map/all_to_all | solution.py:56
  338.5 95.8 %all-to-all-done.2 = bf16[64,2,128,128]{3,2,1,0:T(8,128)(2,1)} async-done(((bf16[64,2,128,128]{3,2,1,0:T(8,128)(2,1)}), bf16[64,2,128,128]{3,2,1,0:T(8,128)(2,1)}, u32[]{:S(2)}, u32[]{:S(2)}) %all-to-all-start.2) | async-done | bytes 4194336 | tf_op jit(solution)/shard_map/all_to_all | solution.py:56
  438.8 28.7 %reduce-scatter.2.cloned.1.call-done = bf16[64,32,128]{2,1,0:T(8,128)(2,1)} async-done(((bf16[64,128,128]{2,1,0:T(8,128)(2,1)}), bf16[64,32,128]{2,1,0:T(8,128)(2,1)}) %reduce-scatter.2.cloned.1.call-update) | async-done | bytes 524304 | tf_op jit(solution)/shard_map/reduce_scatter | solution.py:59
  (52 shorter events, 30.9 us)
Async XLA Ops:
  6.5 188.5 %all-gather.2.cloned.1.call-start = ((), (), s32[]{:S(2)}) async-start(), calls=%async_computation.4 | async-start | bytes 21299200 | tf_op jit(solution)/shard_map/all_gather | solution.py:37
  10.1 28.1 %all-to-all-start.1 = ((s32[64,2,1]{1,2,0:T(1,128)}), s32[64,2,1]{1,2,0:T(1,128)S(1)}, u32[]{:S(2)}, u32[]{:S(2)}) async-start(s32[64,2,1]{1,2,0:T(1,128)} %bitcast.19), calls=%async_computation.1 | async-start | bytes 65536 | tf_op jit(solution)/shard_map/all_to_all | solution.py:48
  38.2 142.2 %all-to-all-start = ((bf16[64,2,128,128]{3,2,1,0:T(8,128)(2,1)}), bf16[64,2,128,128]{3,2,1,0:T(8,128)(2,1)}, u32[]{:S(2)}, u32[]{:S(2)}) async-start(bf16[64,2,128,128]{3,2,1,0:T(8,128)(2,1)} %bitcast.83), calls=%async_computation | async-start | bytes 8388608 | tf_op jit(solution)/shard_map/all_to_all | solution.py:47
  50.1 145.0 %copy-start = (bf16[10,1,128,128]{3,2,1,0:T(8,128)(2,1)S(1)}, bf16[10,1,128,128]{3,2,1,0:T(8,128)(2,1)}, u32[]{:S(2)}) copy-start(bf16[10,1,128,128]{3,2,1,0:T(8,128)(2,1)} %param.10) | copy-start | bytes 983044
  330.8 103.5 %all-to-all-start.2 = ((bf16[64,2,128,128]{3,2,1,0:T(8,128)(2,1)}), bf16[64,2,128,128]{3,2,1,0:T(8,128)(2,1)}, u32[]{:S(2)}, u32[]{:S(2)}) async-start(bf16[64,2,128,128]{3,2,1,0:T(8,128)(2,1)} %bitcast.85), calls=%async_computation.2 | async-start | bytes 8388608 | tf_op jit(solution)/shard_map/all_to_all | solution.py:56
  338.5 129.0 %reduce-scatter.2.cloned.1.call-start = ((), (), s32[]{:S(2)}) async-start(), calls=%async_computation.5 | async-start | bytes 2621440 | tf_op jit(solution)/shard_map/reduce_scatter | solution.py:59
Sparse Core Ops, SparseCore 0:
  10.2 184.8 all-gather.1
  438.8 28.6 reduce-scatter.1
where the time goes:
time: 478 us; the launch traced here: 477 us
  waiting for transfers between devices  264 us (55%)
  local copies, waits for them, and re-layouts  109 us (23%)
  matrix products  51.5 us (11%)
  starting transfers between devices  31.3 us (7%)
  between operations  13.5 us (3%)
  other arithmetic  7.78 us (2%)
    all_to_all x1, waiting for transfers between devices, on_device(): lax.all_to_all(outgoing, 'wave', split_axis=0, concat_axis=0, tiled=True)  130 us
    all_to_all x1, waiting for transfers between devices, on_device(): lax.all_to_all(parts, 'wave', split_axis=0, concat_axis=0, tiled=True)  95.8 us
    gather x8, local copies, waits for them, and re-layouts, slot_work(): chosen = jnp.take(right_all, where, axis=1)  84 us
    dot_general x8, matrix products, slot_work(): jnp.einsum('nwac,wncd->nad', inner, chosen, preferred_element_type=jnp.fl...  51.5 us
    reduce_scatter x1, waiting for transfers between devices, on_device(): lax.psum_scatter(home.astype(jnp.float32).astype(jnp.bfloat16), 'env', sc...  28.7 us
    all_to_all x1, starting transfers between devices, on_device(): lax.all_to_all(places, 'wave', split_axis=0, concat_axis=0, tiled=True)  13.2 us
    all_to_all x1, starting transfers between devices, on_device(): lax.all_to_all(outgoing, 'wave', split_axis=0, concat_axis=0, tiled=True)  10.5 us
  transfers between devices with their start and end apart: 5, of which 4 were waited for; matrix products, arithmetic and copies ran while one was open for 5% of the time, Pallas kernels for 0%

commit v1 on v0

v1 whole, which is shorter than its diff:
```python
import functools

import jax
import jax.numpy as jnp
from jax import lax
from jax.experimental import pallas as pl
from jax.experimental.pallas import tpu as pltpu
from jax.sharding import PartitionSpec as P


def block_kernel(lpos, rpos, lrows, rrows, psi_ref, l_ref, r_ref, out_ref):
    k = pl.program_id(0)
    width = psi_ref.shape[1]
    rows = lax.broadcasted_iota(jnp.int32, (width, width), 0)
    cols = lax.broadcasted_iota(jnp.int32, (width, width), 1)
    mask = (rows < lrows[k]) & (cols < rrows[k])
    masked = jnp.where(mask, psi_ref[0], jnp.zeros_like(psi_ref[0]))
    acc = jnp.zeros((width, width), jnp.float32)
    for w in range(l_ref.shape[0]):
        y = jnp.dot(l_ref[w, 0], masked, preferred_element_type=jnp.float32)
        acc = acc + jnp.dot(y.astype(jnp.bfloat16), r_ref[w, 0], preferred_element_type=jnp.float32)
    out_ref[0] = jnp.where(mask, acc, 0.0).astype(out_ref.dtype)


def apply_blocks(psi, left_all, right_all, lpos, rpos, lrows, rrows):
    count, width, _ = psi.shape
    chans = left_all.shape[0]
    grid_spec = pltpu.PrefetchScalarGridSpec(
        num_scalar_prefetch=4,
        grid=(count,),
        in_specs=[
            pl.BlockSpec((1, width, width), lambda k, lp, rp, lr, rr: (k, 0, 0)),
            pl.BlockSpec((chans, 1, width, width), lambda k, lp, rp, lr, rr: (0, lp[k], 0, 0)),
            pl.BlockSpec((chans, 1, width, width), lambda k, lp, rp, lr, rr: (0, rp[k], 0, 0)),
        ],
        out_specs=pl.BlockSpec((1, width, width), lambda k, lp, rp, lr, rr: (k, 0, 0)),
    )
    flops = count * chans * 4 * width ** 3
    nbytes = count * (2 * chans + 2) * width * width * 2
    return pl.pallas_call(
        block_kernel,
        grid_spec=grid_spec,
        out_shape=jax.ShapeDtypeStruct((count, width, width), jnp.bfloat16),
        cost_estimate=pl.CostEstimate(flops=flops, bytes_accessed=nbytes, transcendentals=0),
    )(lpos, rpos, lrows, rrows, psi, left_all, right_all)


def on_device(psi, left_env, right_env, left_sector, right_sector, sector_owner, sector_rows):
    nenv = lax.axis_size("env")
    count, width, _ = psi.shape
    lsec = left_sector[:, 0]
    rsec = right_sector[:, 0]
    lpos = sector_owner[lsec]
    rpos = sector_owner[rsec]
    lrows = sector_rows[lsec]
    rrows = sector_rows[rsec]
    left_all = lax.all_gather(left_env, "wave", axis=1, tiled=True)
    right_all = lax.all_gather(right_env, "wave", axis=1, tiled=True)
    part = apply_blocks(psi, left_all, right_all, lpos, rpos, lrows, rrows)
    share = width // nenv
    part = part.reshape(count, nenv, share, width)
    got = lax.all_to_all(part, "env", split_axis=1, concat_axis=1, tiled=True)
    total = jnp.sum(got.astype(jnp.float32), axis=1)
    return total.astype(jnp.bfloat16)


def solution(mesh):
    return jax.shard_map(
        on_device,
        mesh=mesh,
        in_specs=(
            P("wave", None, None),
            P("env", "wave", None, None),
            P("env", "wave", None, None),
            P("wave", None),
            P("wave", None),
            P(),
            P(),
        ),
        out_specs=P("wave", "env", None),
        check_vma=False,
    )
```

time: 478 us -> 330 us (0.69)
  local copies, waits for them, and re-layouts: 109 us -> 7.91 us
  Pallas kernels: 0 us -> 53.5 us
  matrix products: 51.5 us -> 0 us
  waiting for transfers between devices: 264 us -> 222 us
  starting transfers between devices: 31.3 us -> 0.04 us
  blocking collectives: 0 us -> 29.7 us
  other arithmetic: 7.78 us -> 2.58 us
    all_to_all x3 -> x0, waiting for transfers between devices: 226 us -> none  [the longest x1 130 us: on_device(): lax.all_to_all(outgoing, 'wave', split_axis=0, concat_axis=0, tiled=True)]
    all_gather x0 -> x1, waiting for transfers between devices: none -> 110 us  [on_device(): left_all = lax.all_gather(left_env, 'wave', axis=1, tiled=True)]
    all_gather x1, waiting for transfers between devices: 8.14 us -> 110 us  [on_device(): right_all = lax.all_gather(right_env, 'wave', axis=1, tiled=True)]
    gather x9 -> x4, local copies, waits for them, and re-layouts: 88.4 us -> 5.92 us  [the longest x1 2.01 us: on_device(): rpos = sector_owner[rsec]]
    pallas_call x0 -> x1, Pallas kernels: none -> 53.5 us  [apply_blocks(): pl.pallas_call(block_kernel, grid_spec=grid_spec, out_shape=jax.ShapeDtyp...]
    dot_general x8 -> x0, matrix products: 51.5 us -> none  [slot_work(): jnp.einsum('nwac,wncd->nad', inner, chosen, preferred_element_type=jnp.fl...]
    all_to_all x3 -> x0, starting transfers between devices: 31.3 us -> none  [the longest x1 13.2 us: on_device(): lax.all_to_all(places, 'wave', split_axis=0, concat_axis=0, tiled=True)]
    all_to_all x0 -> x1, blocking collectives: none -> 29.7 us  [on_device(): got = lax.all_to_all(part, 'env', split_axis=1, concat_axis=1, tiled=True)]
  transfers between devices with their start and end apart: 5 -> 2, of which waited for: 4 -> 2; matrix products, arithmetic and copies ran while one was open for 5% -> 2% of each run, Pallas kernels for 0% -> 0%
where the time goes in v1:
time: 330 us; the launch traced here: 329 us
  waiting for transfers between devices  222 us (67%)
  Pallas kernels  53.5 us (16%)
  blocking collectives  29.7 us (9%)
  between operations  13.4 us (4%)
  local copies, waits for them, and re-layouts  7.91 us (2%)
    all_gather x1, waiting for transfers between devices, on_device(): right_all = lax.all_gather(right_env, 'wave', axis=1, tiled=True)  110 us
    all_gather x1, waiting for transfers between devices, on_device(): left_all = lax.all_gather(left_env, 'wave', axis=1, tiled=True)  110 us
    pallas_call x1, Pallas kernels, apply_blocks(): pl.pallas_call(block_kernel, grid_spec=grid_spec, out_shape=jax.ShapeDtyp...  53.5 us
    all_to_all x1, blocking collectives, on_device(): got = lax.all_to_all(part, 'env', split_axis=1, concat_axis=1, tiled=True)  29.7 us
  transfers between devices with their start and end apart: 2, of which 2 were waited for; matrix products, arithmetic and copies ran while one was open for 2% of the time, Pallas kernels for 0%

profile of v1, /device:TPU:1, one launch (start us, length us, event | category | flops | bytes accessed | tf_op | source)
XLA Modules:
  0.0 328.8 jit_solution(2878252934107693879)
XLA Ops:
  6.5 0.0 copy-start
  6.5 0.0 copy-start.1
  6.5 0.0 all-gather.3.cloned.1.call-start
  6.5 0.7 all-gather.3.cloned.1.call-update
  7.3 0.0 all-gather.5.cloned.1.call-start
  7.3 0.7 all-gather.5.cloned.1.call-update
  8.0 0.7 fusion.1
  8.7 0.0 copy-done
  8.7 1.3 gather_fusion.3
  10.0 2.0 gather_fusion.1
  12.0 0.7 fusion
  12.7 1.3 gather_fusion.2
  14.0 0.0 copy-done.1
  14.0 1.3 gather_fusion
  15.3 109.8 %all-gather.3.cloned.1.call-done.l_ref = bf16[10,64,128,128]{3,2,1,0:T(8,128)(2,1)} async-done(((bf16[10,1,128,128]{3,2,1,0:T(8,128)(2,1)}), bf16[10,64,128,128]{3,2,1,0:T(8,128)(2,1)}) %all-gather.3.cloned.1.call-update) | async-done | bytes 20971536 | tf_op jit(solution)/shard_map/all_gather | solution.py:57
  125.0 110.4 %all-gather.5.cloned.1.call-done.r_ref = bf16[10,64,128,128]{3,2,1,0:T(8,128)(2,1)} async-done(((bf16[10,1,128,128]{3,2,1,0:T(8,128)(2,1)}), bf16[10,64,128,128]{3,2,1,0:T(8,128)(2,1)}) %all-gather.5.cloned.1.call-update) | async-done | bytes 20971536 | tf_op jit(solution)/shard_map/all_gather | solution.py:58
  235.4 53.5 %shard_map.73 = bf16[64,128,128]{2,1,0:T(8,128)(2,1)} custom-call(s32[64]{0:T(128)} %gather_fusion, s32[64]{0:T(128)} %gather_fusion.1, s32[64]{0:T(128)} %gather_fusion.2, s32[64]{0:T(128)} %gather_fusion.3, bf16[64,128,128]{2,1,0:T(8,128)(2,1)} %psi_ref.1, bf16[10,64,128,128]{3,2,1,0:T(8,128)(2,1)} %all-gather.3.cloned.1.call-done.l_ref, ...), custom_call_target="tpu_custom_call" | custom-call | flops 5368709120 | bytes 46137344 | tf_op jit(solution)/shard_map/pallas_call | solution.py:40
  288.9 2.0 copy.8
  290.9 29.7 %all_to_all.5 = bf16[64,4,32,128]{3,2,0,1:T(8,128)(2,1)S(1)} all-to-all(bf16[64,4,32,128]{3,2,0,1:T(8,128)(2,1)S(1)} %copy.8), channel_id=1, replica_groups=mesh['env'=4,'wave'=64] {'env'}, dimensions={1} | all-to-all | bytes 4194304 | tf_op jit(solution)/shard_map/all_to_all | solution.py:62
  320.7 1.2 reduce_sum.12
  (2 shorter events, 0.0 us)
Async XLA Ops:
  6.5 2.1 copy-start
  6.5 7.4 %copy-start.1 = (s32[64]{0:T(128)S(1)}, s32[64]{0:T(128)}, u32[]{:S(2)}) copy-start(s32[64]{0:T(128)} %param.12) | copy-start | bytes 772
  6.5 118.5 %all-gather.3.cloned.1.call-start = ((), (), s32[]{:S(2)}) async-start(), calls=%async_computation.1 | async-start | bytes 21299200 | tf_op jit(solution)/shard_map/all_gather | solution.py:57
  7.3 228.2 %all-gather.5.cloned.1.call-start = ((), (), s32[]{:S(2)}) async-start(), calls=%async_computation.2 | async-start | bytes 21299200 | tf_op jit(solution)/shard_map/all_gather | solution.py:58
Sparse Core Ops, SparseCore 0:
  10.2 114.8 all-gather.2
  127.8 107.5 all-gather.4

commit v2 on v1

--- a/solution.py
+++ b/solution.py
@@ -15,10 +15,12 @@
     cols = lax.broadcasted_iota(jnp.int32, (width, width), 1)
     mask = (rows < lrows[k]) & (cols < rrows[k])
     masked = jnp.where(mask, psi_ref[0], jnp.zeros_like(psi_ref[0]))
-    acc = jnp.zeros((width, width), jnp.float32)
-    for w in range(l_ref.shape[0]):
-        y = jnp.dot(l_ref[w, 0], masked, preferred_element_type=jnp.float32)
-        acc = acc + jnp.dot(y.astype(jnp.bfloat16), r_ref[w, 0], preferred_element_type=jnp.float32)
+    chans = l_ref.shape[0]
+    lmat = l_ref[...].reshape(chans * width, width)
+    y = jnp.dot(lmat, masked, preferred_element_type=jnp.float32).astype(jnp.bfloat16)
+    ywide = jnp.concatenate([y[w * width:(w + 1) * width] for w in range(chans)], axis=1)
+    rmat = r_ref[...].reshape(chans * width, width)
+    acc = jnp.dot(ywide, rmat, preferred_element_type=jnp.float32)
     out_ref[0] = jnp.where(mask, acc, 0.0).astype(out_ref.dtype)
 
 
@@ -45,6 +47,13 @@
     )(lpos, rpos, lrows, rrows, psi, left_all, right_all)
 
 
+def gather_env(env):
+    chans, _, width, _ = env.shape
+    over_chips = lax.all_gather(env, "chip", axis=1, tiled=True)
+    both = lax.all_gather(over_chips, "core", axis=2)
+    return both.reshape(chans, -1, width, width)
+
+
 def on_device(psi, left_env, right_env, left_sector, right_sector, sector_owner, sector_rows):
     nenv = lax.axis_size("env")
     count, width, _ = psi.shape
@@ -54,8 +63,8 @@
     rpos = sector_owner[rsec]
     lrows = sector_rows[lsec]
     rrows = sector_rows[rsec]
-    left_all = lax.all_gather(left_env, "wave", axis=1, tiled=True)
-    right_all = lax.all_gather(right_env, "wave", axis=1, tiled=True)
+    left_all = gather_env(left_env)
+    right_all = gather_env(right_env)
     part = apply_blocks(psi, left_all, right_all, lpos, rpos, lrows, rrows)
     share = width // nenv
     part = part.reshape(count, nenv, share, width)
@@ -65,18 +74,21 @@
 
 
 def solution(mesh):
+    nenv, nwave = mesh.devices.shape
+    split = jax.sharding.Mesh(mesh.devices.reshape(nenv, nwave // 2, 2), ("env", "chip", "core"))
+    wave = ("chip", "core")
     return jax.shard_map(
         on_device,
-        mesh=mesh,
+        mesh=split,
         in_specs=(
-            P("wave", None, None),
-            P("env", "wave", None, None),
-            P("env", "wave", None, None),
-            P("wave", None),
-            P("wave", None),
+            P(wave, None, None),
+            P("env", wave, None, None),
+            P("env", wave, None, None),
+            P(wave, None),
+            P(wave, None),
             P(),
             P(),
         ),
-        out_specs=P("wave", "env", None),
+        out_specs=P(wave, "env", None),
         check_vma=False,
     )

time: 330 us -> 411 us (1.25)
  waiting for transfers between devices: 222 us -> 305 us
    all_gather x2 -> x4, waiting for transfers between devices: 220 us -> 303 us  [the longest x2 223 us: gather_env(): over_chips = lax.all_gather(env, 'chip', axis=1, tiled=True)]
  transfers between devices with their start and end apart: 2 -> 4, of which waited for: 2 -> 4; matrix products, arithmetic and copies ran while one was open for 2% -> 1% of each run, Pallas kernels for 0% -> 0%
where the time goes in v2:
time: 411 us; the launch traced here: 410 us
  waiting for transfers between devices  305 us (74%)
  Pallas kernels  53.5 us (13%)
  blocking collectives  29.6 us (7%)
  between operations  13.2 us (3%)
  local copies, waits for them, and re-layouts  7.24 us (2%)
    all_gather x2, waiting for transfers between devices, gather_env(): over_chips = lax.all_gather(env, 'chip', axis=1, tiled=True)  223 us
    all_gather x2, waiting for transfers between devices, gather_env(): both = lax.all_gather(over_chips, 'core', axis=2)  80.1 us
    pallas_call x1, Pallas kernels, apply_blocks(): pl.pallas_call(block_kernel, grid_spec=grid_spec, out_shape=jax.ShapeDtyp...  53.5 us
    all_to_all x1, blocking collectives, on_device(): got = lax.all_to_all(part, 'env', split_axis=1, concat_axis=1, tiled=True)  29.6 us
  transfers between devices with their start and end apart: 4, of which 4 were waited for; matrix products, arithmetic and copies ran while one was open for 1% of the time, Pallas kernels for 0%

profile of v2, /device:TPU:1, one launch (start us, length us, event | category | flops | bytes accessed | tf_op | source)
XLA Modules:
  0.0 409.6 jit_solution(11814597103580020633)
XLA Ops:
  6.5 0.0 copy-start
  6.5 0.0 all-gather.7.cloned.1.call-start
  6.5 0.7 all-gather.7.cloned.1.call-update
  7.3 0.0 all-gather.9.cloned.1.call-start
  7.3 0.7 all-gather.9.cloned.1.call-update
  8.0 0.0 all-gather.11.cloned.1.call-start
  8.1 114.4 %all-gather.7.cloned.1.call-done = bf16[10,32,128,128]{3,2,1,0:T(8,128)(2,1)} async-done(((bf16[10,1,128,128]{3,2,1,0:T(8,128)(2,1)}), bf16[10,32,128,128]{3,2,1,0:T(8,128)(2,1)}) %all-gather.7.cloned.1.call-update) | async-done | bytes 10485776 | tf_op jit(solution)/shard_map/all_gather | solution.py:52
  122.5 0.0 all-gather.11.cloned.1.call-update
  122.5 0.0 all-gather.13.cloned.1.call-start
  122.6 108.7 %all-gather.9.cloned.1.call-done = bf16[10,32,128,128]{3,2,1,0:T(8,128)(2,1)} async-done(((bf16[10,1,128,128]{3,2,1,0:T(8,128)(2,1)}), bf16[10,32,128,128]{3,2,1,0:T(8,128)(2,1)}) %all-gather.9.cloned.1.call-update) | async-done | bytes 10485776 | tf_op jit(solution)/shard_map/all_gather | solution.py:52
  231.3 0.0 all-gather.13.cloned.1.call-update
  231.3 0.0 copy-done.3
  231.3 0.0 copy-done
  231.3 1.4 gather_fusion.3
  232.7 1.3 gather_fusion.1
  234.0 0.0 copy-done.4
  234.0 1.3 gather_fusion.2
  235.3 1.3 gather_fusion
  236.6 35.9 %all-gather.11.cloned.1.call-done = bf16[10,32,256,128]{3,2,1,0:T(8,128)(2,1)} async-done(((bf16[10,32,128,128]{3,2,1,0:T(8,128)(2,1)}), bf16[10,32,256,128]{3,2,1,0:T(8,128)(2,1)}) %all-gather.11.cloned.1.call-update) | async-done | bytes 20971536 | tf_op jit(solution)/shard_map/all_gather | solution.py:53
  272.5 44.2 %all-gather.13.cloned.1.call-done = bf16[10,32,256,128]{3,2,1,0:T(8,128)(2,1)} async-done(((bf16[10,32,128,128]{3,2,1,0:T(8,128)(2,1)}), bf16[10,32,256,128]{3,2,1,0:T(8,128)(2,1)}) %all-gather.13.cloned.1.call-update) | async-done | bytes 20971536 | tf_op jit(solution)/shard_map/all_gather | solution.py:53
  316.7 53.5 %shard_map.73 = bf16[64,128,128]{2,1,0:T(8,128)(2,1)} custom-call(s32[64]{0:T(128)} %gather_fusion, s32[64]{0:T(128)} %gather_fusion.1, s32[64]{0:T(128)} %gather_fusion.2, s32[64]{0:T(128)} %gather_fusion.3, bf16[64,128,128]{2,1,0:T(8,128)(2,1)} %psi_ref.1, bf16[10,64,128,128]{3,2,1,0:T(8,128)(2,1)} %bitcast.7, bf16[10,64,128,128]{3,2,1,0:T(8,128)(2,1)} %bitcast.8), custom_call_target="tpu_custom_call" | custom-call | flops 5368709120 | bytes 46137344 | tf_op jit(solution)/shard_map/pallas_call | solution.py:42
  370.2 2.0 copy.8
  372.2 29.6 %all_to_all.5 = bf16[64,4,32,128]{3,2,0,1:T(8,128)(2,1)S(1)} all-to-all(bf16[64,4,32,128]{3,2,0,1:T(8,128)(2,1)S(1)} %copy.8), channel_id=1, replica_groups=mesh['env'=4,'chip'=32,'core'=2] {'env'}, dimensions={1} | all-to-all | bytes 4194304 | tf_op jit(solution)/shard_map/all_to_all | solution.py:71
  401.8 1.2 reduce_sum.12
  (10 shorter events, 0.0 us)
Async XLA Ops:
  6.5 224.8 %copy-start = (s32[64]{0:T(128)S(1)}, s32[64]{0:T(128)}, u32[]{:S(2)}) copy-start(s32[64]{0:T(128)} %param.13) | copy-start | bytes 772
  6.5 116.0 %all-gather.7.cloned.1.call-start = ((), (), s32[]{:S(2)}) async-start(), calls=%async_computation.1 | async-start | bytes 10813440 | tf_op jit(solution)/shard_map/all_gather | solution.py:52
  7.3 224.0 %all-gather.9.cloned.1.call-start = ((), (), s32[]{:S(2)}) async-start(), calls=%async_computation.2 | async-start | bytes 10813440 | tf_op jit(solution)/shard_map/all_gather | solution.py:52
  8.0 264.5 %all-gather.11.cloned.1.call-start = ((), (), s32[]{:S(2)}) async-start(), calls=%async_computation.3 | async-start | bytes 31457280 | tf_op jit(solution)/shard_map/all_gather | solution.py:53
  122.5 108.8 %copy-start.3 = (s32[64,1]{0,1:T(1,128)S(1)}, s32[64,1]{0,1:T(1,128)}, u32[]{:S(2)}) copy-start(s32[64,1]{0,1:T(1,128)} %param.11) | copy-start | bytes 772
  122.5 110.2 %copy-start.2 = (s32[64]{0:T(128)S(1)}, s32[64]{0:T(128)}, u32[]{:S(2)}) copy-start(s32[64]{0:T(128)} %param.12) | copy-start | bytes 772
  122.5 111.5 %copy-start.4 = (s32[64,1]{0,1:T(1,128)S(1)}, s32[64,1]{0,1:T(1,128)}, u32[]{:S(2)}) copy-start(s32[64,1]{0,1:T(1,128)} %param.10) | copy-start | bytes 772
  122.5 194.2 %all-gather.13.cloned.1.call-start = ((), (), s32[]{:S(2)}) async-start(), calls=%async_computation.4 | async-start | bytes 31457280 | tf_op jit(solution)/shard_map/all_gather | solution.py:53
  316.7 86.4 %copy-start.1 = (s32[64]{0:T(128)S(1)}, s32[64]{0:T(128)}, u32[]{:S(2)}) copy-start(s32[64]{0:T(128)} %param.13) | copy-start | bytes 772
Sparse Core Ops, SparseCore 0:
  9.9 112.5 all-gather.6
  125.1 106.1 all-gather.8
  233.1 39.3 all-gather.10
  274.2 42.4 all-gather.12

commit v3 on v2

v3 whole, which is shorter than its diff:
```python
import functools

import jax
import jax.numpy as jnp
from jax import lax
from jax.experimental import pallas as pl
from jax.experimental.pallas import tpu as pltpu
from jax.sharding import PartitionSpec as P

MESH = pl.DeviceIdType.MESH
NY, NZ = 4, 8


def gather_kernel(x_ref, g_ref, own_sem, recv, sent):
    e = lax.axis_index("env")
    y = lax.axis_index("y")
    z = lax.axis_index("z")
    c = lax.axis_index("core")

    def dev(yy, zz, cc):
        return (e, lax.rem(yy + NY, NY), lax.rem(zz + NZ, NZ), cc)

    def slot(yy, zz, cc):
        return (lax.rem(yy + NY, NY) * NZ + lax.rem(zz + NZ, NZ)) * 2 + cc

    barrier = pltpu.get_barrier_semaphore()
    peers = [dev(y + 1, z, c), dev(y - 1, z, c), dev(y, z + 1, c), dev(y, z - 1, c), dev(y, z, 1 - c)]
    for p in peers:
        pl.semaphore_signal(barrier, inc=1, device_id=p, device_id_type=MESH)
    pl.semaphore_wait(barrier, len(peers))

    own = pltpu.make_async_copy(x_ref, g_ref.at[slot(y, z, c)], own_sem)
    own.start()

    def role(cc, first, second):
        fsize, fstep = first
        ssize, sstep = second
        fplus, fminus = fsize // 2, fsize - 1 - fsize // 2
        splus, sminus = ssize // 2, ssize - 1 - ssize // 2
        sends = []

        def origin(a, b):
            fy, fz = fstep(a)
            sy, sz = sstep(b)
            return y - fy - sy, z - fz - sz

        def send(src, a, b, target, kind):
            oy, oz = origin(a, b)
            s = slot(oy, oz, cc)
            cp = pltpu.make_async_remote_copy(
                src_ref=src, dst_ref=g_ref.at[s], send_sem=sent.at[s, kind],
                recv_sem=recv.at[s], device_id=target, device_id_type=MESH)
            cp.start()
            sends.append(cp)

        def wait_in(a, b):
            oy, oz = origin(a, b)
            s = slot(oy, oz, cc)
            cp = pltpu.make_async_remote_copy(
                src_ref=g_ref.at[s], dst_ref=g_ref.at[s], send_sem=sent.at[s, 0],
                recv_sem=recv.at[s], device_id=dev(y, z, 1 - cc), device_id_type=MESH)
            cp.wait_recv()

        def held(a, b):
            oy, oz = origin(a, b)
            return g_ref.at[slot(oy, oz, cc)]

        fp_y, fp_z = fstep(1)
        sp_y, sp_z = sstep(1)
        f_next, f_prev = dev(y + fp_y, z + fp_z, cc), dev(y - fp_y, z - fp_z, cc)
        s_next, s_prev = dev(y + sp_y, z + sp_z, cc), dev(y - sp_y, z - sp_z, cc)
        partner = dev(y, z, 1 - cc)

        def spread(src, a, b):
            if b == 0:
                send(src, a, 0, s_next, 2)
                send(src, a, 0, s_prev, 3)
            elif 0 < b < splus:
                send(src, a, b, s_next, 2)
            elif 0 < -b < sminus:
                send(src, a, b, s_prev, 3)
            send(src, a, b, partner, 4)

        send(x_ref, 0, 0, f_next, 0)
        send(x_ref, 0, 0, f_prev, 1)
        spread(x_ref, 0, 0)
        for step in range(1, max(fplus, fminus) + 1):
            for a in (step, -step):
                if (a > 0 and a > fplus) or (a < 0 and -a > fminus):
                    continue
                wait_in(a, 0)
                if 0 < a < fplus:
                    send(held(a, 0), a, 0, f_next, 0)
                if 0 < -a < fminus:
                    send(held(a, 0), a, 0, f_prev, 1)
                spread(held(a, 0), a, 0)
        row = list(range(-fminus, fplus + 1))
        for step in range(1, max(splus, sminus) + 1):
            for b in (step, -step):
                if (b > 0 and b > splus) or (b < 0 and -b > sminus):
                    continue
                for a in row:
                    wait_in(a, b)
                    spread(held(a, b), a, b)
        for yy in range(NY):
            for zz in range(NZ):
                s = (yy * NZ + zz) * 2 + (1 - cc)
                cp = pltpu.make_async_remote_copy(
                    src_ref=g_ref.at[s], dst_ref=g_ref.at[s], send_sem=sent.at[s, 0],
                    recv_sem=recv.at[s], device_id=partner, device_id_type=MESH)
                cp.wait_recv()
        for cp in sends:
            cp.wait_send()

    zstep = lambda d: (0, d)
    ystep = lambda d: (d, 0)

    @pl.when(c == 0)
    def _():
        role(0, (NZ, zstep), (NY, ystep))

    @pl.when(c == 1)
    def _():
        role(1, (NY, ystep), (NZ, zstep))

    own.wait()


def gather_env(x):
    shape = (NY * NZ * 2,) + x.shape
    return pl.pallas_call(
        gather_kernel,
        out_shape=jax.ShapeDtypeStruct(shape, x.dtype),
        in_specs=[pl.BlockSpec(memory_space=pl.ANY)],
        out_specs=pl.BlockSpec(memory_space=pl.ANY),
        scratch_shapes=[
            pltpu.SemaphoreType.DMA(()),
            pltpu.SemaphoreType.DMA((NY * NZ * 2,)),
            pltpu.SemaphoreType.DMA((NY * NZ * 2, 5)),
        ],
        compiler_params=pltpu.CompilerParams(collective_id=0, has_side_effects=True),
    )(x)


def block_kernel(lpos, rpos, lrows, rrows, psi_ref, l_ref, r_ref, out_ref):
    k = pl.program_id(0)
    width = psi_ref.shape[1]
    rows = lax.broadcasted_iota(jnp.int32, (width, width), 0)
    cols = lax.broadcasted_iota(jnp.int32, (width, width), 1)
    mask = (rows < lrows[k]) & (cols < rrows[k])
    masked = jnp.where(mask, psi_ref[0], jnp.zeros_like(psi_ref[0]))
    chans = l_ref.shape[1]
    lmat = l_ref[...].reshape(chans * width, width)
    y = jnp.dot(lmat, masked, preferred_element_type=jnp.float32).astype(jnp.bfloat16)
    ywide = jnp.concatenate([y[w * width:(w + 1) * width] for w in range(chans)], axis=1)
    rmat = r_ref[...].reshape(chans * width, width)
    acc = jnp.dot(ywide, rmat, preferred_element_type=jnp.float32)
    out_ref[0] = jnp.where(mask, acc, 0.0).astype(out_ref.dtype)


def apply_blocks(psi, both, lpos, rpos, lrows, rrows):
    count, width, _ = psi.shape
    chans = both.shape[1] // 2
    grid_spec = pltpu.PrefetchScalarGridSpec(
        num_scalar_prefetch=4,
        grid=(count,),
        in_specs=[
            pl.BlockSpec((1, width, width), lambda k, lp, rp, lr, rr: (k, 0, 0)),
            pl.BlockSpec((1, chans, width, width), lambda k, lp, rp, lr, rr: (lp[k], 0, 0, 0)),
            pl.BlockSpec((1, chans, width, width), lambda k, lp, rp, lr, rr: (rp[k], 1, 0, 0)),
        ],
        out_specs=pl.BlockSpec((1, width, width), lambda k, lp, rp, lr, rr: (k, 0, 0)),
    )
    flops = count * chans * 4 * width ** 3
    nbytes = count * (2 * chans + 2) * width * width * 2
    return pl.pallas_call(
        block_kernel,
        grid_spec=grid_spec,
        out_shape=jax.ShapeDtypeStruct((count, width, width), jnp.bfloat16),
        cost_estimate=pl.CostEstimate(flops=flops, bytes_accessed=nbytes, transcendentals=0),
    )(lpos, rpos, lrows, rrows, psi, both, both)


def on_device(psi, left_env, right_env, left_sector, right_sector, sector_owner, sector_rows):
    nenv = lax.axis_size("env")
    count, width, _ = psi.shape
    lsec = left_sector[:, 0]
    rsec = right_sector[:, 0]
    lpos = sector_owner[lsec]
    rpos = sector_owner[rsec]
    lrows = sector_rows[lsec]
    rrows = sector_rows[rsec]
    both = gather_env(jnp.concatenate([left_env[:, 0], right_env[:, 0]], axis=0))
    part = apply_blocks(psi, both, lpos, rpos, lrows, rrows)
    share = width // nenv
    part = part.reshape(count, nenv, share, width)
    got = lax.all_to_all(part, "env", split_axis=1, concat_axis=1, tiled=True)
    total = jnp.sum(got.astype(jnp.float32), axis=1)
    return total.astype(jnp.bfloat16)


def solution(mesh):
    nenv, nwave = mesh.devices.shape
    split = jax.sharding.Mesh(mesh.devices.reshape(nenv, NY, NZ, 2), ("env", "y", "z", "core"))
    wave = ("y", "z", "core")
    return jax.shard_map(
        on_device,
        mesh=split,
        in_specs=(
            P(wave, None, None),
            P("env", wave, None, None),
            P("env", wave, None, None),
            P(wave, None),
            P(wave, None),
            P(),
            P(),
        ),
        out_specs=P(wave, "env", None),
        check_vma=False,
    )
```

time: 411 us -> 253 us (0.62)
  waiting for transfers between devices: 305 us -> 0 us
  Pallas kernels: 53.5 us -> 211 us
  between operations: 13.2 us -> 0.03 us
    all_gather x4 -> x0, waiting for transfers between devices: 303 us -> none  [the longest x2 223 us: gather_env(): over_chips = lax.all_gather(env, 'chip', axis=1, tiled=True)]
    pallas_call x0 -> x1, Pallas kernels: none -> 157 us  [gather_env(): pl.pallas_call(gather_kernel, out_shape=jax.ShapeDtypeStruct(shape, x.dty...]
  transfers between devices with their start and end apart: 4 -> 0, of which waited for: 4 -> 0; matrix products, arithmetic and copies ran while one was open for 1% -> 0% of each run, Pallas kernels for 0% -> 0%
where the time goes in v3:
time: 253 us; the launch traced here: 252 us
  Pallas kernels  211 us (83%)
  blocking collectives  29.2 us (12%)
  local copies, waits for them, and re-layouts  8.5 us (3%)
  other arithmetic  3.57 us (1%)
    pallas_call x1, Pallas kernels, gather_env(): pl.pallas_call(gather_kernel, out_shape=jax.ShapeDtypeStruct(shape, x.dty...  157 us
    pallas_call x1, Pallas kernels, apply_blocks(): pl.pallas_call(block_kernel, grid_spec=grid_spec, out_shape=jax.ShapeDtyp...  53.2 us
    all_to_all x1, blocking collectives, on_device(): got = lax.all_to_all(part, 'env', split_axis=1, concat_axis=1, tiled=True)  29.2 us

profile of v3, /device:TPU:1, one launch (start us, length us, event | category | flops | bytes accessed | tf_op | source)
XLA Modules:
  0.0 251.9 jit_solution(6959648889836328558)
XLA Ops:
  0.0 0.0 copy-start
  0.0 0.0 copy-start.1
  0.0 0.0 copy-start.2
  0.0 0.7 fusion
  0.7 0.7 fusion.1
  1.4 0.0 copy-done
  1.4 1.3 gather_fusion.3
  2.7 2.0 gather_fusion.1
  4.6 1.3 gather_fusion.2
  6.0 1.9 gather_fusion
  7.9 0.0 copy-done.1
  7.9 0.0 copy-done.2
  7.9 0.9 pad_maximum_fusion.x_ref
  8.8 157.4 %shard_map.73.l_ref.r_ref = bf16[64,20,128,128]{3,2,1,0:T(8,128)(2,1)} custom-call(bf16[20,128,128]{2,1,0:T(8,128)(2,1)} %pad_maximum_fusion.x_ref), custom_call_target="tpu_custom_call" | custom-call | tf_op jit(solution)/shard_map/pallas_call | solution.py:131
  166.3 53.2 %shard_map.74 = bf16[64,128,128]{2,1,0:T(8,128)(2,1)} custom-call(s32[64]{0:T(128)} %gather_fusion, s32[64]{0:T(128)} %gather_fusion.1, s32[64]{0:T(128)} %gather_fusion.2, s32[64]{0:T(128)} %gather_fusion.3, bf16[64,128,128]{2,1,0:T(8,128)(2,1)} %psi_ref.1, bf16[64,20,128,128]{3,2,1,0:T(8,128)(2,1)} %shard_map.73.l_ref.r_ref, ...), custom_call_target="tpu_custom_call" | custom-call | flops 5368709120 | bytes 46137344 | tf_op jit(solution)/shard_map/pallas_call | solution.py:176
  219.5 2.0 copy.8
  221.5 29.2 %all_to_all.5 = bf16[64,4,32,128]{3,2,0,1:T(8,128)(2,1)S(1)} all-to-all(bf16[64,4,32,128]{3,2,0,1:T(8,128)(2,1)S(1)} %copy.8), channel_id=1, replica_groups=mesh['env'=4,'y'=4,'z'=8,'core'=2] {'env'}, dimensions={1} | all-to-all | bytes 4194304 | tf_op jit(solution)/shard_map/all_to_all | solution.py:197
  250.7 1.2 reduce_sum.12
  (2 shorter events, 0.0 us)
Async XLA Ops:
  0.0 1.4 copy-start
  0.0 7.9 %copy-start.1 = (bf16[10,1,128,128]{3,2,1,0:T(8,128)(2,1)S(1)}, bf16[10,1,128,128]{3,2,1,0:T(8,128)(2,1)}, u32[]{:S(2)}) copy-start(bf16[10,1,128,128]{3,2,1,0:T(8,128)(2,1)} %param.9) | copy-start | bytes 983044
  0.0 7.9 %copy-start.2 = (bf16[10,1,128,128]{3,2,1,0:T(8,128)(2,1)S(1)}, bf16[10,1,128,128]{3,2,1,0:T(8,128)(2,1)}, u32[]{:S(2)}) copy-start(bf16[10,1,128,128]{3,2,1,0:T(8,128)(2,1)} %param.8) | copy-start | bytes 983044

commit v4 on v3

--- a/solution.py
+++ b/solution.py
@@ -142,12 +142,12 @@
     )(x)
 
 
-def block_kernel(lpos, rpos, lrows, rrows, psi_ref, l_ref, r_ref, out_ref):
-    k = pl.program_id(0)
+def block_kernel(base, lsec, rsec, owner, live, psi_ref, l_ref, r_ref, out_ref):
+    k = pl.program_id(0) + base
     width = psi_ref.shape[1]
     rows = lax.broadcasted_iota(jnp.int32, (width, width), 0)
     cols = lax.broadcasted_iota(jnp.int32, (width, width), 1)
-    mask = (rows < lrows[k]) & (cols < rrows[k])
+    mask = (rows < live[lsec[k]]) & (cols < live[rsec[k]])
     masked = jnp.where(mask, psi_ref[0], jnp.zeros_like(psi_ref[0]))
     chans = l_ref.shape[1]
     lmat = l_ref[...].reshape(chans * width, width)
@@ -155,48 +155,46 @@
     ywide = jnp.concatenate([y[w * width:(w + 1) * width] for w in range(chans)], axis=1)
     rmat = r_ref[...].reshape(chans * width, width)
     acc = jnp.dot(ywide, rmat, preferred_element_type=jnp.float32)
-    out_ref[0] = jnp.where(mask, acc, 0.0).astype(out_ref.dtype)
-
-
-def apply_blocks(psi, both, lpos, rpos, lrows, rrows):
+    part = jnp.where(mask, acc, 0.0).astype(jnp.bfloat16)
+    out_ref[0] = part.astype(out_ref.dtype)
+
+
+def apply_blocks(psi, both, lsec, rsec, owner, live, base, size):
     count, width, _ = psi.shape
     chans = both.shape[1] // 2
     grid_spec = pltpu.PrefetchScalarGridSpec(
         num_scalar_prefetch=4,
-        grid=(count,),
+        grid=(size,),
         in_specs=[
-            pl.BlockSpec((1, width, width), lambda k, lp, rp, lr, rr: (k, 0, 0)),
-            pl.BlockSpec((1, chans, width, width), lambda k, lp, rp, lr, rr: (lp[k], 0, 0, 0)),
-            pl.BlockSpec((1, chans, width, width), lambda k, lp, rp, lr, rr: (rp[k], 1, 0, 0)),
+            pl.BlockSpec((1, width, width), lambda k, ls, rs, ow, lv: (k + base, 0, 0)),
+            pl.BlockSpec((1, chans, width, width), lambda k, ls, rs, ow, lv: (ow[ls[k + base]], 0, 0, 0)),
+            pl.BlockSpec((1, chans, width, width), lambda k, ls, rs, ow, lv: (ow[rs[k + base]], 1, 0, 0)),
         ],
-        out_specs=pl.BlockSpec((1, width, width), lambda k, lp, rp, lr, rr: (k, 0, 0)),
+        out_specs=pl.BlockSpec((1, width, width), lambda k, ls, rs, ow, lv: (k, 0, 0)),
     )
-    flops = count * chans * 4 * width ** 3
-    nbytes = count * (2 * chans + 2) * width * width * 2
+    flops = size * chans * 4 * width ** 3
+    nbytes = size * (2 * chans + 3) * width * width * 2
     return pl.pallas_call(
-        block_kernel,
+        functools.partial(block_kernel, base),
         grid_spec=grid_spec,
-        out_shape=jax.ShapeDtypeStruct((count, width, width), jnp.bfloat16),
+        out_shape=jax.ShapeDtypeStruct((size, width, width), jnp.float32),
         cost_estimate=pl.CostEstimate(flops=flops, bytes_accessed=nbytes, transcendentals=0),
-    )(lpos, rpos, lrows, rrows, psi, both, both)
+    )(lsec, rsec, owner, live, psi, both, both)
 
 
 def on_device(psi, left_env, right_env, left_sector, right_sector, sector_owner, sector_rows):
-    nenv = lax.axis_size("env")
     count, width, _ = psi.shape
     lsec = left_sector[:, 0]
     rsec = right_sector[:, 0]
-    lpos = sector_owner[lsec]
-    rpos = sector_owner[rsec]
-    lrows = sector_rows[lsec]
-    rrows = sector_rows[rsec]
     both = gather_env(jnp.concatenate([left_env[:, 0], right_env[:, 0]], axis=0))
-    part = apply_blocks(psi, both, lpos, rpos, lrows, rrows)
-    share = width // nenv
-    part = part.reshape(count, nenv, share, width)
-    got = lax.all_to_all(part, "env", split_axis=1, concat_axis=1, tiled=True)
-    total = jnp.sum(got.astype(jnp.float32), axis=1)
-    return total.astype(jnp.bfloat16)
+    pieces = 4
+    size = count // pieces
+    outs = []
+    for i in range(pieces):
+        part = apply_blocks(psi, both, lsec, rsec, sector_owner, sector_rows, i * size, size)
+        total = lax.psum_scatter(part, "env", scatter_dimension=1, tiled=True)
+        outs.append(total.astype(jnp.bfloat16))
+    return jnp.concatenate(outs, axis=0)
 
 
 def solution(mesh):

time: 253 us -> 298 us (1.18)
  waiting for transfers between devices: 0 us -> 59.1 us
  blocking collectives: 29.2 us -> 0 us
  between operations: 0.03 us -> 13.2 us
  local copies, waits for them, and re-layouts: 8.5 us -> 0 us
  Pallas kernels: 211 us -> 217 us
  other arithmetic: 3.57 us -> 6.74 us
    reduce_scatter x0 -> x4, waiting for transfers between devices: none -> 59 us  [on_device(): total = lax.psum_scatter(part, 'env', scatter_dimension=1, tiled=True)]
    all_to_all x1 -> x0, blocking collectives: 29.2 us -> none  [on_device(): got = lax.all_to_all(part, 'env', split_axis=1, concat_axis=1, tiled=True)]
    gather x4 -> x0, local copies, waits for them, and re-layouts: 6.5 us -> none  [the longest x1 1.96 us: on_device(): rpos = sector_owner[rsec]]
    pallas_call x1 -> x4, Pallas kernels: 53.2 us -> 59.7 us  [apply_blocks(): pl.pallas_call(functools.partial(block_kernel, base), grid_spec=grid_spec...]
    convert_element_type x0 -> x4, other arithmetic: none -> 3.88 us  [on_device(): outs.append(total.astype(jnp.bfloat16))]
  transfers between devices with their start and end apart: 0 -> 4, of which waited for: 0 -> 3; matrix products, arithmetic and copies ran while one was open for 0% -> 1% of each run, Pallas kernels for 0% -> 15%
where the time goes in v4:
time: 298 us; the launch traced here: 296 us
  Pallas kernels  217 us (73%)
  waiting for transfers between devices  59.1 us (20%)
  between operations  13.2 us (4%)
  other arithmetic  6.74 us (2%)
    pallas_call x1, Pallas kernels, gather_env(): pl.pallas_call(gather_kernel, out_shape=jax.ShapeDtypeStruct(shape, x.dty...  157 us
    pallas_call x4, Pallas kernels, apply_blocks(): pl.pallas_call(functools.partial(block_kernel, base), grid_spec=grid_spec...  59.7 us
    reduce_scatter x4, waiting for transfers between devices, on_device(): total = lax.psum_scatter(part, 'env', scatter_dimension=1, tiled=True)  59 us
  transfers between devices with their start and end apart: 4, of which 3 were waited for; matrix products, arithmetic and copies ran while one was open for 1% of the time, Pallas kernels for 15%

profile of v4, /device:TPU:1, one launch (start us, length us, event | category | flops | bytes accessed | tf_op | source)
XLA Modules:
  0.0 296.3 jit_solution(12489111581015411271)
XLA Ops:
  6.5 0.0 reduce-scatter.5.cloned.1.call-start
  6.5 2.0 pad_maximum_fusion.x_ref
  8.5 157.4 %shard_map.73.l_ref.r_ref = bf16[64,20,128,128]{3,2,1,0:T(8,128)(2,1)} custom-call(bf16[20,128,128]{2,1,0:T(8,128)(2,1)} %pad_maximum_fusion.x_ref), custom_call_target="tpu_custom_call" | custom-call | tf_op jit(solution)/shard_map/pallas_call | solution.py:131
  166.0 14.9 %shard_map.74 = f32[16,128,128]{2,1,0:T(8,128)} custom-call(s32[64]{0:T(128)} %bitcast.6, s32[64]{0:T(128)} %bitcast.10, s32[64]{0:T(128)} %owner.7, s32[64]{0:T(128)} %live.7, bf16[64,128,128]{2,1,0:T(8,128)(2,1)} %psi_ref.7, bf16[64,20,128,128]{3,2,1,0:T(8,128)(2,1)} %shard_map.73.l_ref.r_ref, bf16[64,20,128,128]{3,2,1,0:T(8,128)(2,1)} %shard_map.73.l_ref.r_ref), custom_call_target="tpu_custom_call" | custom-call | flops 1342177280 | bytes 12058624 | tf_op jit(solution)/shard_map/pallas_call | solution.py:177
  180.9 0.0 reduce-scatter.5.cloned.1.call-update
  180.9 0.0 reduce-scatter.7.cloned.1.call-start
  180.9 15.0 %shard_map.75 = f32[16,128,128]{2,1,0:T(8,128)} custom-call(s32[64]{0:T(128)} %bitcast.7, s32[64]{0:T(128)} %bitcast.11, s32[64]{0:T(128)} %owner.7, s32[64]{0:T(128)} %live.7, bf16[64,128,128]{2,1,0:T(8,128)(2,1)} %psi_ref.7, bf16[64,20,128,128]{3,2,1,0:T(8,128)(2,1)} %shard_map.73.l_ref.r_ref, bf16[64,20,128,128]{3,2,1,0:T(8,128)(2,1)} %shard_map.73.l_ref.r_ref), custom_call_target="tpu_custom_call" | custom-call | flops 1342177280 | bytes 12058624 | tf_op jit(solution)/shard_map/pallas_call | solution.py:177
  195.9 0.0 reduce-scatter.7.cloned.1.call-update
  195.9 0.0 reduce-scatter.9.cloned.1.call-start
  196.0 14.9 %shard_map.76 = f32[16,128,128]{2,1,0:T(8,128)} custom-call(s32[64]{0:T(128)} %bitcast.8, s32[64]{0:T(128)} %bitcast.12, s32[64]{0:T(128)} %owner.7, s32[64]{0:T(128)} %live.7, bf16[64,128,128]{2,1,0:T(8,128)(2,1)} %psi_ref.7, bf16[64,20,128,128]{3,2,1,0:T(8,128)(2,1)} %shard_map.73.l_ref.r_ref, bf16[64,20,128,128]{3,2,1,0:T(8,128)(2,1)} %shard_map.73.l_ref.r_ref), custom_call_target="tpu_custom_call" | custom-call | flops 1342177280 | bytes 12058624 | tf_op jit(solution)/shard_map/pallas_call | solution.py:177
  210.9 0.0 reduce-scatter.9.cloned.1.call-update
  210.9 0.0 reduce-scatter.11.cloned.1.call-start
  210.9 15.0 %shard_map.77 = f32[16,128,128]{2,1,0:T(8,128)} custom-call(s32[64]{0:T(128)} %bitcast.9, s32[64]{0:T(128)} %bitcast.13, s32[64]{0:T(128)} %owner.7, s32[64]{0:T(128)} %live.7, bf16[64,128,128]{2,1,0:T(8,128)(2,1)} %psi_ref.7, bf16[64,20,128,128]{3,2,1,0:T(8,128)(2,1)} %shard_map.73.l_ref.r_ref, bf16[64,20,128,128]{3,2,1,0:T(8,128)(2,1)} %shard_map.73.l_ref.r_ref), custom_call_target="tpu_custom_call" | custom-call | flops 1342177280 | bytes 12058624 | tf_op jit(solution)/shard_map/pallas_call | solution.py:177
  226.0 0.0 reduce-scatter.11.cloned.1.call-update
  226.0 0.0 reduce-scatter.5.cloned.1.call-done
  226.0 1.0 convert_element_type.12
  227.0 4.1 %reduce-scatter.7.cloned.1.call-done = f32[16,32,128]{2,1,0:T(8,128)} async-done(((f32[16,128,128]{2,1,0:T(8,128)}), f32[16,32,128]{2,1,0:T(8,128)}) %reduce-scatter.7.cloned.1.call-update) | async-done | bytes 262160 | tf_op jit(solution)/shard_map/reduce_scatter | solution.py:195
  231.1 1.0 convert_element_type.13
  232.1 27.4 %reduce-scatter.9.cloned.1.call-done = f32[16,32,128]{2,1,0:T(8,128)} async-done(((f32[16,128,128]{2,1,0:T(8,128)}), f32[16,32,128]{2,1,0:T(8,128)}) %reduce-scatter.9.cloned.1.call-update) | async-done | bytes 262160 | tf_op jit(solution)/shard_map/reduce_scatter | solution.py:195
  259.5 1.0 convert_element_type.14
  260.5 27.5 %reduce-scatter.11.cloned.1.call-done = f32[16,32,128]{2,1,0:T(8,128)} async-done(((f32[16,128,128]{2,1,0:T(8,128)}), f32[16,32,128]{2,1,0:T(8,128)}) %reduce-scatter.11.cloned.1.call-update) | async-done | bytes 262160 | tf_op jit(solution)/shard_map/reduce_scatter | solution.py:195
  287.9 1.0 convert_element_type.15
  288.9 0.9 pad_maximum_fusion.1
Async XLA Ops:
  6.5 219.5 %reduce-scatter.5.cloned.1.call-start = ((), (), s32[]{:S(2)}) async-start(), calls=%async_computation.4 | async-start | bytes 1310720 | tf_op jit(solution)/shard_map/reduce_scatter | solution.py:195
  180.9 50.2 %reduce-scatter.7.cloned.1.call-start = ((), (), s32[]{:S(2)}) async-start(), calls=%async_computation.5 | async-start | bytes 1310720 | tf_op jit(solution)/shard_map/reduce_scatter | solution.py:195
  195.9 63.6 %reduce-scatter.9.cloned.1.call-start = ((), (), s32[]{:S(2)}) async-start(), calls=%async_computation.6 | async-start | bytes 1310720 | tf_op jit(solution)/shard_map/reduce_scatter | solution.py:195
  210.9 77.0 %reduce-scatter.11.cloned.1.call-start = ((), (), s32[]{:S(2)}) async-start(), calls=%async_computation.7 | async-start | bytes 1310720 | tf_op jit(solution)/shard_map/reduce_scatter | solution.py:195
Sparse Core Ops, SparseCore 0:
  181.0 21.4 reduce-scatter.4
  205.2 25.8 reduce-scatter.6
  233.6 25.8 reduce-scatter.8
  262.1 25.8 reduce-scatter.10

commit v5 on v3

--- a/solution.py
+++ b/solution.py
@@ -142,12 +142,12 @@
     )(x)
 
 
-def block_kernel(lpos, rpos, lrows, rrows, psi_ref, l_ref, r_ref, out_ref):
-    k = pl.program_id(0)
+def block_kernel(order, lsec, rsec, owner, live, psi_ref, l_ref, r_ref, out_ref):
+    k = order[pl.program_id(0)]
     width = psi_ref.shape[1]
     rows = lax.broadcasted_iota(jnp.int32, (width, width), 0)
     cols = lax.broadcasted_iota(jnp.int32, (width, width), 1)
-    mask = (rows < lrows[k]) & (cols < rrows[k])
+    mask = (rows < live[lsec[k]]) & (cols < live[rsec[k]])
     masked = jnp.where(mask, psi_ref[0], jnp.zeros_like(psi_ref[0]))
     chans = l_ref.shape[1]
     lmat = l_ref[...].reshape(chans * width, width)
@@ -158,18 +158,18 @@
     out_ref[0] = jnp.where(mask, acc, 0.0).astype(out_ref.dtype)
 
 
-def apply_blocks(psi, both, lpos, rpos, lrows, rrows):
+def apply_blocks(psi, both, order, lsec, rsec, owner, live):
     count, width, _ = psi.shape
     chans = both.shape[1] // 2
     grid_spec = pltpu.PrefetchScalarGridSpec(
-        num_scalar_prefetch=4,
+        num_scalar_prefetch=5,
         grid=(count,),
         in_specs=[
-            pl.BlockSpec((1, width, width), lambda k, lp, rp, lr, rr: (k, 0, 0)),
-            pl.BlockSpec((1, chans, width, width), lambda k, lp, rp, lr, rr: (lp[k], 0, 0, 0)),
-            pl.BlockSpec((1, chans, width, width), lambda k, lp, rp, lr, rr: (rp[k], 1, 0, 0)),
+            pl.BlockSpec((1, width, width), lambda i, od, ls, rs, ow, lv: (od[i], 0, 0)),
+            pl.BlockSpec((1, chans, width, width), lambda i, od, ls, rs, ow, lv: (ow[ls[od[i]]], 0, 0, 0)),
+            pl.BlockSpec((1, chans, width, width), lambda i, od, ls, rs, ow, lv: (ow[rs[od[i]]], 1, 0, 0)),
         ],
-        out_specs=pl.BlockSpec((1, width, width), lambda k, lp, rp, lr, rr: (k, 0, 0)),
+        out_specs=pl.BlockSpec((1, width, width), lambda i, od, ls, rs, ow, lv: (od[i], 0, 0)),
     )
     flops = count * chans * 4 * width ** 3
     nbytes = count * (2 * chans + 2) * width * width * 2
@@ -178,7 +178,15 @@
         grid_spec=grid_spec,
         out_shape=jax.ShapeDtypeStruct((count, width, width), jnp.bfloat16),
         cost_estimate=pl.CostEstimate(flops=flops, bytes_accessed=nbytes, transcendentals=0),
-    )(lpos, rpos, lrows, rrows, psi, both, both)
+    )(order, lsec, rsec, owner, live, psi, both, both)
+
+
+def by_left_sector(lsec):
+    count = lsec.shape[0]
+    pos = jnp.arange(count, dtype=jnp.int32)
+    before = (lsec[None, :] < lsec[:, None]) | ((lsec[None, :] == lsec[:, None]) & (pos[None, :] < pos[:, None]))
+    rank = jnp.sum(before.astype(jnp.int32), axis=1)
+    return jnp.sum(jnp.where(rank[None, :] == pos[:, None], pos[None, :], 0), axis=1)
 
 
 def on_device(psi, left_env, right_env, left_sector, right_sector, sector_owner, sector_rows):
@@ -186,12 +194,9 @@
     count, width, _ = psi.shape
     lsec = left_sector[:, 0]
     rsec = right_sector[:, 0]
-    lpos = sector_owner[lsec]
-    rpos = sector_owner[rsec]
-    lrows = sector_rows[lsec]
-    rrows = sector_rows[rsec]
+    order = by_left_sector(lsec)
     both = gather_env(jnp.concatenate([left_env[:, 0], right_env[:, 0]], axis=0))
-    part = apply_blocks(psi, both, lpos, rpos, lrows, rrows)
+    part = apply_blocks(psi, both, order, lsec, rsec, sector_owner, sector_rows)
     share = width // nenv
     part = part.reshape(count, nenv, share, width)
     got = lax.all_to_all(part, "env", split_axis=1, concat_axis=1, tiled=True)

time: 253 us -> 248 us (0.980)
  local copies, waits for them, and re-layouts: 8.5 us -> 1.99 us
    gather x4 -> x0, local copies, waits for them, and re-layouts: 6.5 us -> none  [the longest x1 1.96 us: on_device(): rpos = sector_owner[rsec]]
where the time goes in v5:
time: 248 us; the launch traced here: 247 us
  Pallas kernels  210 us (85%)
  blocking collectives  29.3 us (12%)
  other arithmetic  4.78 us (2%)
    pallas_call x1, Pallas kernels, gather_env(): pl.pallas_call(gather_kernel, out_shape=jax.ShapeDtypeStruct(shape, x.dty...  157 us
    pallas_call x1, Pallas kernels, apply_blocks(): pl.pallas_call(block_kernel, grid_spec=grid_spec, out_shape=jax.ShapeDtyp...  53 us
    all_to_all x1, blocking collectives, on_device(): got = lax.all_to_all(part, 'env', split_axis=1, concat_axis=1, tiled=True)  29.3 us

profile of v5, /device:TPU:1, one launch (start us, length us, event | category | flops | bytes accessed | tf_op | source)
XLA Modules:
  0.0 246.6 jit_solution(10815785147353844962)
XLA Ops:
  0.0 0.9 convert_reduce_fusion
  0.9 0.6 select_reduce_fusion.order
  1.6 2.0 pad_maximum_fusion.x_ref
  3.5 157.4 %shard_map.73.l_ref.r_ref = bf16[64,20,128,128]{3,2,1,0:T(8,128)(2,1)} custom-call(bf16[20,128,128]{2,1,0:T(8,128)(2,1)} %pad_maximum_fusion.x_ref), custom_call_target="tpu_custom_call" | custom-call | tf_op jit(solution)/shard_map/pallas_call | solution.py:131
  161.0 53.0 %shard_map.74 = bf16[64,128,128]{2,1,0:T(8,128)(2,1)} custom-call(s32[64]{0:T(128)} %select_reduce_fusion.order, s32[64]{0:T(128)} %bitcast.9, s32[64]{0:T(128)} %bitcast.10, s32[64]{0:T(128)} %owner.1, s32[64]{0:T(128)} %live.1, bf16[64,128,128]{2,1,0:T(8,128)(2,1)} %psi_ref.1, bf16[64,20,128,128]{3,2,1,0:T(8,128)(2,1)} %shard_map.73.l_ref.r_ref, ...), custom_call_target="tpu_custom_call" | custom-call | flops 5368709120 | bytes 46137344 | tf_op jit(solution)/shard_map/pallas_call | solution.py:176
  214.0 2.0 copy.9
  216.0 29.3 %all_to_all.5 = bf16[64,4,32,128]{3,2,0,1:T(8,128)(2,1)S(1)} all-to-all(bf16[64,4,32,128]{3,2,0,1:T(8,128)(2,1)S(1)} %copy.9), channel_id=1, replica_groups=mesh['env'=4,'y'=4,'z'=8,'core'=2] {'env'}, dimensions={1} | all-to-all | bytes 4194304 | tf_op jit(solution)/shard_map/all_to_all | solution.py:202
  245.3 1.2 reduce_sum.32

commit v6 on v5

--- a/solution.py
+++ b/solution.py
@@ -16,12 +16,13 @@
     y = lax.axis_index("y")
     z = lax.axis_index("z")
     c = lax.axis_index("core")
+    half = x_ref.shape[0] // 2
 
     def dev(yy, zz, cc):
-        return (e, lax.rem(yy + NY, NY), lax.rem(zz + NZ, NZ), cc)
+        return (e, lax.rem(yy + 2 * NY, NY), lax.rem(zz + 2 * NZ, NZ), cc)
 
     def slot(yy, zz, cc):
-        return (lax.rem(yy + NY, NY) * NZ + lax.rem(zz + NZ, NZ)) * 2 + cc
+        return (lax.rem(yy + 2 * NY, NY) * NZ + lax.rem(zz + 2 * NZ, NZ)) * 2 + cc
 
     barrier = pltpu.get_barrier_semaphore()
     peers = [dev(y + 1, z, c), dev(y - 1, z, c), dev(y, z + 1, c), dev(y, z - 1, c), dev(y, z, 1 - c)]
@@ -38,77 +39,82 @@
         fplus, fminus = fsize // 2, fsize - 1 - fsize // 2
         splus, sminus = ssize // 2, ssize - 1 - ssize // 2
         sends = []
-
-        def origin(a, b):
-            fy, fz = fstep(a)
-            sy, sz = sstep(b)
+        partner = dev(y, z, 1 - cc)
+
+        def where(a, b, h):
+            sign = 1 - 2 * h
+            fy, fz = fstep(sign * a)
+            sy, sz = sstep(sign * b)
             return y - fy - sy, z - fz - sz
 
-        def send(src, a, b, target, kind):
-            oy, oz = origin(a, b)
-            s = slot(oy, oz, cc)
+        def part(ref, h):
+            return ref.at[pl.ds(h * half, half)]
+
+        def item(a, b, h):
+            oy, oz = where(a, b, h)
+            return slot(oy, oz, cc)
+
+        def near(h, ring, d):
+            sign = 1 - 2 * h
+            dy, dz = ring(sign * d)
+            return dev(y + dy, z + dz, cc)
+
+        def send(src, a, b, h, target, kind):
+            s = item(a, b, h)
             cp = pltpu.make_async_remote_copy(
-                src_ref=src, dst_ref=g_ref.at[s], send_sem=sent.at[s, kind],
-                recv_sem=recv.at[s], device_id=target, device_id_type=MESH)
+                src_ref=src, dst_ref=part(g_ref.at[s], h), send_sem=sent.at[s, h, kind],
+                recv_sem=recv.at[s, h], device_id=target, device_id_type=MESH)
             cp.start()
             sends.append(cp)
 
-        def wait_in(a, b):
-            oy, oz = origin(a, b)
-            s = slot(oy, oz, cc)
+        def wait_in(s, h):
             cp = pltpu.make_async_remote_copy(
-                src_ref=g_ref.at[s], dst_ref=g_ref.at[s], send_sem=sent.at[s, 0],
-                recv_sem=recv.at[s], device_id=dev(y, z, 1 - cc), device_id_type=MESH)
+                src_ref=part(g_ref.at[s], h), dst_ref=part(g_ref.at[s], h), send_sem=sent.at[s, h, 0],
+                recv_sem=recv.at[s, h], device_id=partner, device_id_type=MESH)
             cp.wait_recv()
 
-        def held(a, b):
-            oy, oz = origin(a, b)
-            return g_ref.at[slot(oy, oz, cc)]
-
-        fp_y, fp_z = fstep(1)
-        sp_y, sp_z = sstep(1)
-        f_next, f_prev = dev(y + fp_y, z + fp_z, cc), dev(y - fp_y, z - fp_z, cc)
-        s_next, s_prev = dev(y + sp_y, z + sp_z, cc), dev(y - sp_y, z - sp_z, cc)
-        partner = dev(y, z, 1 - cc)
-
-        def spread(src, a, b):
+        def held(a, b, h):
+            return part(g_ref.at[item(a, b, h)], h)
+
+        def spread(src, a, b, h):
             if b == 0:
-                send(src, a, 0, s_next, 2)
-                send(src, a, 0, s_prev, 3)
+                send(src, a, 0, h, near(h, sstep, 1), 2)
+                send(src, a, 0, h, near(h, sstep, -1), 3)
             elif 0 < b < splus:
-                send(src, a, b, s_next, 2)
+                send(src, a, b, h, near(h, sstep, 1), 2)
             elif 0 < -b < sminus:
-                send(src, a, b, s_prev, 3)
-            send(src, a, b, partner, 4)
-
-        send(x_ref, 0, 0, f_next, 0)
-        send(x_ref, 0, 0, f_prev, 1)
-        spread(x_ref, 0, 0)
+                send(src, a, b, h, near(h, sstep, -1), 3)
+            send(src, a, b, h, partner, 4)
+
+        for h in range(2):
+            send(part(x_ref, h), 0, 0, h, near(h, fstep, 1), 0)
+            send(part(x_ref, h), 0, 0, h, near(h, fstep, -1), 1)
+        for h in range(2):
+            spread(part(x_ref, h), 0, 0, h)
         for step in range(1, max(fplus, fminus) + 1):
             for a in (step, -step):
                 if (a > 0 and a > fplus) or (a < 0 and -a > fminus):
                     continue
-                wait_in(a, 0)
-                if 0 < a < fplus:
-                    send(held(a, 0), a, 0, f_next, 0)
-                if 0 < -a < fminus:
-                    send(held(a, 0), a, 0, f_prev, 1)
-                spread(held(a, 0), a, 0)
+                for h in range(2):
+                    wait_in(item(a, 0, h), h)
+                    if 0 < a < fplus:
+                        send(held(a, 0, h), a, 0, h, near(h, fstep, 1), 0)
+                    if 0 < -a < fminus:
+                        send(held(a, 0, h), a, 0, h, near(h, fstep, -1), 1)
+                    spread(held(a, 0, h), a, 0, h)
         row = list(range(-fminus, fplus + 1))
         for step in range(1, max(splus, sminus) + 1):
             for b in (step, -step):
                 if (b > 0 and b > splus) or (b < 0 and -b > sminus):
                     continue
                 for a in row:
-                    wait_in(a, b)
-                    spread(held(a, b), a, b)
+                    for h in range(2):
+                        wait_in(item(a, b, h), h)
+                        spread(held(a, b, h), a, b, h)
         for yy in range(NY):
             for zz in range(NZ):
-                s = (yy * NZ + zz) * 2 + (1 - cc)
-                cp = pltpu.make_async_remote_copy(
-                    src_ref=g_ref.at[s], dst_ref=g_ref.at[s], send_sem=sent.at[s, 0],
-                    recv_sem=recv.at[s], device_id=partner, device_id_type=MESH)
-                cp.wait_recv()
+                for h in range(2):
+                    wait_in((yy * NZ + zz) * 2 + (1 - cc), h)
         for cp in sends:
             cp.wait_send()
 
@@ -135,8 +141,8 @@
         out_specs=pl.BlockSpec(memory_space=pl.ANY),
         scratch_shapes=[
             pltpu.SemaphoreType.DMA(()),
-            pltpu.SemaphoreType.DMA((NY * NZ * 2,)),
-            pltpu.SemaphoreType.DMA((NY * NZ * 2, 5)),
+            pltpu.SemaphoreType.DMA((NY * NZ * 2, 2)),
+            pltpu.SemaphoreType.DMA((NY * NZ * 2, 2, 5)),
         ],
         compiler_params=pltpu.CompilerParams(collective_id=0, has_side_effects=True),
     )(x)

time: 248 us -> 233 us (0.940)
  Pallas kernels: 210 us -> 195 us
    pallas_call x1, Pallas kernels: 157 us -> 142 us  [gather_env(): pl.pallas_call(gather_kernel, out_shape=jax.ShapeDtypeStruct(shape, x.dty...]
where the time goes in v6:
time: 233 us; the launch traced here: 231 us
  Pallas kernels  195 us (84%)
  blocking collectives  29.2 us (13%)
  other arithmetic  4.78 us (2%)
    pallas_call x1, Pallas kernels, gather_env(): pl.pallas_call(gather_kernel, out_shape=jax.ShapeDtypeStruct(shape, x.dty...  142 us
    pallas_call x1, Pallas kernels, apply_blocks(): pl.pallas_call(block_kernel, grid_spec=grid_spec, out_shape=jax.ShapeDtyp...  53.1 us
    all_to_all x1, blocking collectives, on_device(): got = lax.all_to_all(part, 'env', split_axis=1, concat_axis=1, tiled=True)  29.2 us

profile of v6, /device:TPU:1, one launch (start us, length us, event | category | flops | bytes accessed | tf_op | source)
XLA Modules:
  0.0 231.4 jit_solution(9865215101785548884)
XLA Ops:
  0.0 0.9 convert_reduce_fusion
  0.9 0.6 select_reduce_fusion.order
  1.6 2.0 pad_maximum_fusion.x_ref
  3.5 142.3 %shard_map.73.l_ref.r_ref = bf16[64,20,128,128]{3,2,1,0:T(8,128)(2,1)} custom-call(bf16[20,128,128]{2,1,0:T(8,128)(2,1)} %pad_maximum_fusion.x_ref), custom_call_target="tpu_custom_call" | custom-call | tf_op jit(solution)/shard_map/pallas_call | solution.py:137
  145.9 53.1 %shard_map.74 = bf16[64,128,128]{2,1,0:T(8,128)(2,1)} custom-call(s32[64]{0:T(128)} %select_reduce_fusion.order, s32[64]{0:T(128)} %bitcast.9, s32[64]{0:T(128)} %bitcast.10, s32[64]{0:T(128)} %owner.1, s32[64]{0:T(128)} %live.1, bf16[64,128,128]{2,1,0:T(8,128)(2,1)} %psi_ref.1, bf16[64,20,128,128]{3,2,1,0:T(8,128)(2,1)} %shard_map.73.l_ref.r_ref, ...), custom_call_target="tpu_custom_call" | custom-call | flops 5368709120 | bytes 46137344 | tf_op jit(solution)/shard_map/pallas_call | solution.py:182
  199.0 2.0 copy.9
  201.0 29.2 %all_to_all.5 = bf16[64,4,32,128]{3,2,0,1:T(8,128)(2,1)S(1)} all-to-all(bf16[64,4,32,128]{3,2,0,1:T(8,128)(2,1)S(1)} %copy.9), channel_id=1, replica_groups=mesh['env'=4,'y'=4,'z'=8,'core'=2] {'env'}, dimensions={1} | all-to-all | bytes 4194304 | tf_op jit(solution)/shard_map/all_to_all | solution.py:208
  230.2 1.2 reduce_sum.32

commit v7 on v6

--- a/solution.py
+++ b/solution.py
@@ -148,34 +148,40 @@
     )(x)
 
 
-def block_kernel(order, lsec, rsec, owner, live, psi_ref, l_ref, r_ref, out_ref):
-    k = order[pl.program_id(0)]
+def block_kernel(lsec, rsec, owner, live, psi_ref, *refs):
+    group = psi_ref.shape[0]
     width = psi_ref.shape[1]
+    env_refs, out_ref = refs[:-1], refs[-1]
     rows = lax.broadcasted_iota(jnp.int32, (width, width), 0)
     cols = lax.broadcasted_iota(jnp.int32, (width, width), 1)
-    mask = (rows < live[lsec[k]]) & (cols < live[rsec[k]])
-    masked = jnp.where(mask, psi_ref[0], jnp.zeros_like(psi_ref[0]))
-    chans = l_ref.shape[1]
-    lmat = l_ref[...].reshape(chans * width, width)
-    y = jnp.dot(lmat, masked, preferred_element_type=jnp.float32).astype(jnp.bfloat16)
-    ywide = jnp.concatenate([y[w * width:(w + 1) * width] for w in range(chans)], axis=1)
-    rmat = r_ref[...].reshape(chans * width, width)
-    acc = jnp.dot(ywide, rmat, preferred_element_type=jnp.float32)
-    out_ref[0] = jnp.where(mask, acc, 0.0).astype(out_ref.dtype)
-
-
-def apply_blocks(psi, both, order, lsec, rsec, owner, live):
+    for j in range(group):
+        k = pl.program_id(0) * group + j
+        l_ref, r_ref = env_refs[2 * j], env_refs[2 * j + 1]
+        mask = (rows < live[lsec[k]]) & (cols < live[rsec[k]])
+        masked = jnp.where(mask, psi_ref[j], jnp.zeros_like(psi_ref[j]))
+        chans = l_ref.shape[1]
+        lmat = l_ref[...].reshape(chans * width, width)
+        y = jnp.dot(lmat, masked, preferred_element_type=jnp.float32).astype(jnp.bfloat16)
+        ywide = jnp.concatenate([y[w * width:(w + 1) * width] for w in range(chans)], axis=1)
+        rmat = r_ref[...].reshape(chans * width, width)
+        acc = jnp.dot(ywide, rmat, preferred_element_type=jnp.float32)
+        out_ref[j] = jnp.where(mask, acc, 0.0).astype(out_ref.dtype)
+
+
+def apply_blocks(psi, both, lsec, rsec, owner, live, group=4):
     count, width, _ = psi.shape
     chans = both.shape[1] // 2
+    env_specs = []
+    for j in range(group):
+        env_specs.append(pl.BlockSpec(
+            (1, chans, width, width), lambda i, ls, rs, ow, lv, j=j: (ow[ls[i * group + j]], 0, 0, 0)))
+        env_specs.append(pl.BlockSpec(
+            (1, chans, width, width), lambda i, ls, rs, ow, lv, j=j: (ow[rs[i * group + j]], 1, 0, 0)))
     grid_spec = pltpu.PrefetchScalarGridSpec(
-        num_scalar_prefetch=5,
-        grid=(count,),
-        in_specs=[
-            pl.BlockSpec((1, width, width), lambda i, od, ls, rs, ow, lv: (od[i], 0, 0)),
-            pl.BlockSpec((1, chans, width, width), lambda i, od, ls, rs, ow, lv: (ow[ls[od[i]]], 0, 0, 0)),
-            pl.BlockSpec((1, chans, width, width), lambda i, od, ls, rs, ow, lv: (ow[rs[od[i]]], 1, 0, 0)),
-        ],
-        out_specs=pl.BlockSpec((1, width, width), lambda i, od, ls, rs, ow, lv: (od[i], 0, 0)),
+        num_scalar_prefetch=4,
+        grid=(count // group,),
+        in_specs=[pl.BlockSpec((group, width, width), lambda i, ls, rs, ow, lv: (i, 0, 0))] + env_specs,
+        out_specs=pl.BlockSpec((group, width, width), lambda i, ls, rs, ow, lv: (i, 0, 0)),
     )
     flops = count * chans * 4 * width ** 3
     nbytes = count * (2 * chans + 2) * width * width * 2
@@ -184,15 +190,7 @@
         grid_spec=grid_spec,
         out_shape=jax.ShapeDtypeStruct((count, width, width), jnp.bfloat16),
         cost_estimate=pl.CostEstimate(flops=flops, bytes_accessed=nbytes, transcendentals=0),
-    )(order, lsec, rsec, owner, live, psi, both, both)
-
-
-def by_left_sector(lsec):
-    count = lsec.shape[0]
-    pos = jnp.arange(count, dtype=jnp.int32)
-    before = (lsec[None, :] < lsec[:, None]) | ((lsec[None, :] == lsec[:, None]) & (pos[None, :] < pos[:, None]))
-    rank = jnp.sum(before.astype(jnp.int32), axis=1)
-    return jnp.sum(jnp.where(rank[None, :] == pos[:, None], pos[None, :], 0), axis=1)
+    )(lsec, rsec, owner, live, psi, *([both] * (2 * group)))
 
 
 def on_device(psi, left_env, right_env, left_sector, right_sector, sector_owner, sector_rows):
@@ -200,9 +198,8 @@
     count, width, _ = psi.shape
     lsec = left_sector[:, 0]
     rsec = right_sector[:, 0]
-    order = by_left_sector(lsec)
     both = gather_env(jnp.concatenate([left_env[:, 0], right_env[:, 0]], axis=0))
-    part = apply_blocks(psi, both, order, lsec, rsec, sector_owner, sector_rows)
+    part = apply_blocks(psi, both, lsec, rsec, sector_owner, sector_rows)
     share = width // nenv
     part = part.reshape(count, nenv, share, width)
     got = lax.all_to_all(part, "env", split_axis=1, concat_axis=1, tiled=True)

time: 233 us -> 204 us (0.88)
  Pallas kernels: 195 us -> 168 us
    pallas_call x1, Pallas kernels: 53.1 us -> 26 us  [apply_blocks(): pl.pallas_call(block_kernel, grid_spec=grid_spec, out_shape=jax.ShapeDtyp...]
where the time goes in v7:
time: 204 us
  Pallas kernels  168 us (82%)
  blocking collectives  30.1 us (15%)
  other arithmetic  3.23 us (2%)
    pallas_call x1, Pallas kernels, gather_env(): pl.pallas_call(gather_kernel, out_shape=jax.ShapeDtypeStruct(shape, x.dty...  142 us
    all_to_all x1, blocking collectives, on_device(): got = lax.all_to_all(part, 'env', split_axis=1, concat_axis=1, tiled=True)  30.1 us
    pallas_call x1, Pallas kernels, apply_blocks(): pl.pallas_call(block_kernel, grid_spec=grid_spec, out_shape=jax.ShapeDtyp...  26 us

profile of v7, /device:TPU:1, one launch (start us, length us, event | category | flops | bytes accessed | tf_op | source)
XLA Modules:
  0.0 203.6 jit_solution(11600838619228579484)
XLA Ops:
  0.0 2.0 pad_maximum_fusion.x_ref
  2.0 142.3 %shard_map.73.refs_0_.refs_1_.refs_2_.refs_3_.refs_4_.refs_5_.refs_6_.refs_7_ = bf16[64,20,128,128]{3,2,1,0:T(8,128)(2,1)} custom-call(bf16[20,128,128]{2,1,0:T(8,128)(2,1)} %pad_maximum_fusion.x_ref), custom_call_target="tpu_custom_call" | custom-call | tf_op jit(solution)/shard_map/pallas_call | solution.py:137
  144.3 26.0 %shard_map.74 = bf16[64,128,128]{2,1,0:T(8,128)(2,1)} custom-call(s32[64]{0:T(128)} %bitcast.8, s32[64]{0:T(128)} %bitcast.9, s32[64]{0:T(128)} %owner.1, s32[64]{0:T(128)} %live.1, bf16[64,128,128]{2,1,0:T(8,128)(2,1)} %psi_ref.1, bf16[64,20,128,128]{3,2,1,0:T(8,128)(2,1)} %shard_map.73.refs_0_.refs_1_.refs_2_.refs_3_.refs_4_.refs_5_.refs_6_.refs_7_, ...), custom_call_target="tpu_custom_call" | custom-call | flops 5368709120 | bytes 46137344 | tf_op jit(solution)/shard_map/pallas_call | solution.py:188
  170.3 2.0 copy.8
  172.3 30.1 %all_to_all.5 = bf16[64,4,32,128]{3,2,0,1:T(8,128)(2,1)S(1)} all-to-all(bf16[64,4,32,128]{3,2,0,1:T(8,128)(2,1)S(1)} %copy.8), channel_id=1, replica_groups=mesh['env'=4,'y'=4,'z'=8,'core'=2] {'env'}, dimensions={1} | all-to-all | bytes 4194304 | tf_op jit(solution)/shard_map/all_to_all | solution.py:205
  202.3 1.2 reduce_sum.12

commit v8 on v7

--- a/solution.py
+++ b/solution.py
@@ -11,12 +11,13 @@
 NY, NZ = 4, 8
 
 
-def gather_kernel(x_ref, g_ref, own_sem, recv, sent):
+def gather_kernel(l_ref, r_ref, g_ref, own_sem, recv, sent):
     e = lax.axis_index("env")
     y = lax.axis_index("y")
     z = lax.axis_index("z")
     c = lax.axis_index("core")
-    half = x_ref.shape[0] // 2
+    half = l_ref.shape[0]
+    shards = (l_ref, r_ref)
 
     def dev(yy, zz, cc):
         return (e, lax.rem(yy + 2 * NY, NY), lax.rem(zz + 2 * NZ, NZ), cc)
@@ -30,8 +31,11 @@
         pl.semaphore_signal(barrier, inc=1, device_id=p, device_id_type=MESH)
     pl.semaphore_wait(barrier, len(peers))
 
-    own = pltpu.make_async_copy(x_ref, g_ref.at[slot(y, z, c)], own_sem)
-    own.start()
+    owns = []
+    for h in range(2):
+        cp = pltpu.make_async_copy(shards[h], g_ref.at[slot(y, z, c), pl.ds(h * half, half)], own_sem.at[h])
+        cp.start()
+        owns.append(cp)
 
     def role(cc, first, second):
         fsize, fstep = first
@@ -87,10 +91,10 @@
             send(src, a, b, h, partner, 4)
 
         for h in range(2):
-            send(part(x_ref, h), 0, 0, h, near(h, fstep, 1), 0)
-            send(part(x_ref, h), 0, 0, h, near(h, fstep, -1), 1)
+            send(shards[h], 0, 0, h, near(h, fstep, 1), 0)
+            send(shards[h], 0, 0, h, near(h, fstep, -1), 1)
         for h in range(2):
-            spread(part(x_ref, h), 0, 0, h)
+            spread(shards[h], 0, 0, h)
         for step in range(1, max(fplus, fminus) + 1):
             for a in (step, -step):
                 if (a > 0 and a > fplus) or (a < 0 and -a > fminus):
@@ -129,23 +133,24 @@
     def _():
         role(1, (NY, ystep), (NZ, zstep))
 
-    own.wait()
-
-
-def gather_env(x):
-    shape = (NY * NZ * 2,) + x.shape
+    for cp in owns:
+        cp.wait()
+
+
+def gather_env(left, right):
+    shape = (NY * NZ * 2, 2 * left.shape[0]) + left.shape[1:]
     return pl.pallas_call(
         gather_kernel,
-        out_shape=jax.ShapeDtypeStruct(shape, x.dtype),
-        in_specs=[pl.BlockSpec(memory_space=pl.ANY)],
+        out_shape=jax.ShapeDtypeStruct(shape, left.dtype),
+        in_specs=[pl.BlockSpec(memory_space=pl.ANY)] * 2,
         out_specs=pl.BlockSpec(memory_space=pl.ANY),
         scratch_shapes=[
-            pltpu.SemaphoreType.DMA(()),
+            pltpu.SemaphoreType.DMA((2,)),
             pltpu.SemaphoreType.DMA((NY * NZ * 2, 2)),
             pltpu.SemaphoreType.DMA((NY * NZ * 2, 2, 5)),
         ],
         compiler_params=pltpu.CompilerParams(collective_id=0, has_side_effects=True),
-    )(x)
+    )(left, right)
 
 
 def block_kernel(lsec, rsec, owner, live, psi_ref, *refs):
@@ -168,7 +173,7 @@
         out_ref[j] = jnp.where(mask, acc, 0.0).astype(out_ref.dtype)
 
 
-def apply_blocks(psi, both, lsec, rsec, owner, live, group=4):
+def apply_blocks(psi, both, lsec, rsec, owner, live, group=8):
     count, width, _ = psi.shape
     chans = both.shape[1] // 2
     env_specs = []
@@ -198,7 +203,7 @@
     count, width, _ = psi.shape
     lsec = left_sector[:, 0]
     rsec = right_sector[:, 0]
-    both = gather_env(jnp.concatenate([left_env[:, 0], right_env[:, 0]], axis=0))
+    both = gather_env(left_env[:, 0], right_env[:, 0])
     part = apply_blocks(psi, both, lsec, rsec, sector_owner, sector_rows)
     share = width // nenv
     part = part.reshape(count, nenv, share, width)

time: 204 us -> 200 us (0.980)
  no operation moved by 1% of the time
where the time goes in v8:
time: 200 us
  Pallas kernels  166 us (83%)
  blocking collectives  30 us (15%)
    pallas_call x1, Pallas kernels, gather_env(): pl.pallas_call(gather_kernel, out_shape=jax.ShapeDtypeStruct(shape, left....  142 us
    all_to_all x1, blocking collectives, on_device(): got = lax.all_to_all(part, 'env', split_axis=1, concat_axis=1, tiled=True)  30 us
    pallas_call x1, Pallas kernels, apply_blocks(): pl.pallas_call(block_kernel, grid_spec=grid_spec, out_shape=jax.ShapeDtyp...  24.1 us

profile of v8, /device:TPU:1, one launch (start us, length us, event | category | flops | bytes accessed | tf_op | source)
XLA Modules:
  0.0 199.6 jit_solution(12041360912005505818)
XLA Ops:
  0.0 142.3 %shard_map.73.refs_0_.refs_1_.refs_2_.refs_3_.refs_4_.refs_5_.refs_6_.refs_7_.refs_8_.refs_9_.refs_10_.refs_11_.refs_12_.refs_13_.refs_14_.refs_15_ = bf16[64,20,128,128]{3,2,1,0:T(8,128)(2,1)} custom-call(bf16[10,128,128]{2,1,0:T(8,128)(2,1)} %bitcast.6, bf16[10,128,128]{2,1,0:T(8,128)(2,1)} %bitcast.7), custom_call_target="tpu_custom_call" | custom-call | tf_op jit(solution)/shard_map/pallas_call | solution.py:142
  142.3 24.1 %shard_map.74 = bf16[64,128,128]{2,1,0:T(8,128)(2,1)} custom-call(s32[64]{0:T(128)} %bitcast.8, s32[64]{0:T(128)} %bitcast.9, s32[64]{0:T(128)} %owner.1, s32[64]{0:T(128)} %live.1, bf16[64,128,128]{2,1,0:T(8,128)(2,1)} %psi_ref.1, ...), custom_call_target="tpu_custom_call" | custom-call | flops 5368709120 | bytes 46137344 | tf_op jit(solution)/shard_map/pallas_call | solution.py:193
  166.4 2.0 copy.8
  168.4 30.0 %all_to_all.5 = bf16[64,4,32,128]{3,2,0,1:T(8,128)(2,1)S(1)} all-to-all(bf16[64,4,32,128]{3,2,0,1:T(8,128)(2,1)S(1)} %copy.8), channel_id=1, replica_groups=mesh['env'=4,'y'=4,'z'=8,'core'=2] {'env'}, dimensions={1} | all-to-all | bytes 4194304 | tf_op jit(solution)/shard_map/all_to_all | solution.py:210
  198.4 1.2 reduce_sum.12

commit v9 on v8

--- a/solution.py
+++ b/solution.py
@@ -170,11 +170,15 @@
         ywide = jnp.concatenate([y[w * width:(w + 1) * width] for w in range(chans)], axis=1)
         rmat = r_ref[...].reshape(chans * width, width)
         acc = jnp.dot(ywide, rmat, preferred_element_type=jnp.float32)
-        out_ref[j] = jnp.where(mask, acc, 0.0).astype(out_ref.dtype)
-
-
-def apply_blocks(psi, both, lsec, rsec, owner, live, group=8):
+        part = jnp.where(mask, acc, 0.0).astype(out_ref.dtype)
+        share = out_ref.shape[2]
+        for r in range(out_ref.shape[0]):
+            out_ref[r, j] = part[r * share:(r + 1) * share]
+
+
+def apply_blocks(psi, both, lsec, rsec, owner, live, nenv, group=8):
     count, width, _ = psi.shape
+    share = width // nenv
     chans = both.shape[1] // 2
     env_specs = []
     for j in range(group):
@@ -186,16 +190,95 @@
         num_scalar_prefetch=4,
         grid=(count // group,),
         in_specs=[pl.BlockSpec((group, width, width), lambda i, ls, rs, ow, lv: (i, 0, 0))] + env_specs,
-        out_specs=pl.BlockSpec((group, width, width), lambda i, ls, rs, ow, lv: (i, 0, 0)),
+        out_specs=pl.BlockSpec((nenv, group, share, width), lambda i, ls, rs, ow, lv: (0, i, 0, 0)),
     )
     flops = count * chans * 4 * width ** 3
     nbytes = count * (2 * chans + 2) * width * width * 2
     return pl.pallas_call(
         block_kernel,
         grid_spec=grid_spec,
-        out_shape=jax.ShapeDtypeStruct((count, width, width), jnp.bfloat16),
+        out_shape=jax.ShapeDtypeStruct((nenv, count, share, width), jnp.bfloat16),
         cost_estimate=pl.CostEstimate(flops=flops, bytes_accessed=nbytes, transcendentals=0),
     )(lsec, rsec, owner, live, psi, *([both] * (2 * group)))
+
+
+def exchange_kernel(part_ref, out_ref, got, relay, own_sem, recv_sem, relay_sem, sent):
+    nenv, count, share, width = part_ref.shape
+    e = lax.axis_index("env")
+    y = lax.axis_index("y")
+    z = lax.axis_index("z")
+    c = lax.axis_index("core")
+    half = count // 2
+
+    def at(d):
+        return lax.rem(e + d + 2 * nenv, nenv)
+
+    def dev(d):
+        return (at(d), y, z, c)
+
+    barrier = pltpu.get_barrier_semaphore()
+    for d in (1, -1):
+        pl.semaphore_signal(barrier, inc=1, device_id=dev(d), device_id_type=MESH)
+    pl.semaphore_wait(barrier, 2)
+
+    own = pltpu.make_async_copy(part_ref.at[e], got.at[e], own_sem)
+    own.start()
+
+    def remote(src, dst, rsem, ssem, d):
+        return pltpu.make_async_remote_copy(
+            src_ref=src, dst_ref=dst, send_sem=ssem, recv_sem=rsem,
+            device_id=dev(d), device_id_type=MESH)
+
+    lo, hi = pl.ds(0, half), pl.ds(half, half)
+    sends = [
+        remote(part_ref.at[at(1)], got.at[e], recv_sem.at[0], sent.at[0], 1),
+        remote(part_ref.at[at(-1)], got.at[e], recv_sem.at[1], sent.at[1], -1),
+        remote(part_ref.at[at(2), lo], relay.at[0], relay_sem.at[0], sent.at[2], 1),
+        remote(part_ref.at[at(2), hi], relay.at[1], relay_sem.at[1], sent.at[3], -1),
+    ]
+    for cp in sends:
+        cp.start()
+    remote(relay.at[0], relay.at[0], relay_sem.at[0], sent.at[2], 1).wait_recv()
+    fwd_up = remote(relay.at[0], got.at[at(-1), lo], recv_sem.at[2], sent.at[4], 1)
+    fwd_up.start()
+    remote(relay.at[1], relay.at[1], relay_sem.at[1], sent.at[3], -1).wait_recv()
+    fwd_down = remote(relay.at[1], got.at[at(1), hi], recv_sem.at[3], sent.at[5], -1)
+    fwd_down.start()
+    remote(got.at[at(-1)], got.at[at(-1)], recv_sem.at[0], sent.at[0], -1).wait_recv()
+    remote(got.at[at(1)], got.at[at(1)], recv_sem.at[1], sent.at[1], 1).wait_recv()
+    remote(got.at[at(2), lo], got.at[at(2), lo], recv_sem.at[2], sent.at[4], -1).wait_recv()
+    remote(got.at[at(2), hi], got.at[at(2), hi], recv_sem.at[3], sent.at[5], 1).wait_recv()
+    own.wait()
+    for cp in sends + [fwd_up, fwd_down]:
+        cp.wait_send()
+
+    def body(j, carry):
+        total = got[0, j].astype(jnp.float32)
+        for s in range(1, nenv):
+            total = total + got[s, j].astype(jnp.float32)
+        out_ref[j] = total.astype(out_ref.dtype)
+        return carry
+
+    lax.fori_loop(0, count, body, 0)
+
+
+def exchange(part):
+    nenv, count, share, width = part.shape
+    return pl.pallas_call(
+        exchange_kernel,
+        out_shape=jax.ShapeDtypeStruct((count, share, width), part.dtype),
+        in_specs=[pl.BlockSpec(memory_space=pl.ANY)],
+        out_specs=pl.BlockSpec(memory_space=pltpu.VMEM),
+        scratch_shapes=[
+            pltpu.VMEM((nenv, count, share, width), part.dtype),
+            pltpu.VMEM((2, count // 2, share, width), part.dtype),
+            pltpu.SemaphoreType.DMA(()),
+            pltpu.SemaphoreType.DMA((4,)),
+            pltpu.SemaphoreType.DMA((2,)),
+            pltpu.SemaphoreType.DMA((6,)),
+        ],
+        compiler_params=pltpu.CompilerParams(collective_id=1, has_side_effects=True),
+    )(part)
 
 
 def on_device(psi, left_env, right_env, left_sector, right_sector, sector_owner, sector_rows):
@@ -204,12 +287,8 @@
     lsec = left_sector[:, 0]
     rsec = right_sector[:, 0]
     both = gather_env(left_env[:, 0], right_env[:, 0])
-    part = apply_blocks(psi, both, lsec, rsec, sector_owner, sector_rows)
-    share = width // nenv
-    part = part.reshape(count, nenv, share, width)
-    got = lax.all_to_all(part, "env", split_axis=1, concat_axis=1, tiled=True)
-    total = jnp.sum(got.astype(jnp.float32), axis=1)
-    return total.astype(jnp.bfloat16)
+    part = apply_blocks(psi, both, lsec, rsec, sector_owner, sector_rows, nenv)
+    return exchange(part)
 
 
 def solution(mesh):

time: 200 us -> 196 us (0.980)
  the two profiles are of different devices: /device:TPU:1 before, /device:TPU:16 now
where the time goes in v9:
time: 196 us
  Pallas kernels  194 us (99%)
    pallas_call x1, Pallas kernels, gather_env(): pl.pallas_call(gather_kernel, out_shape=jax.ShapeDtypeStruct(shape, left....  140 us
    pallas_call x1, Pallas kernels, exchange(): pl.pallas_call(exchange_kernel, out_shape=jax.ShapeDtypeStruct((count, sh...  31 us
    pallas_call x1, Pallas kernels, apply_blocks(): pl.pallas_call(block_kernel, grid_spec=grid_spec, out_shape=jax.ShapeDtyp...  23.6 us

profile of v9, /device:TPU:16, one launch (start us, length us, event | category | flops | bytes accessed | tf_op | source)
XLA Modules:
  0.0 196.3 jit_solution(5044126809725942954)
XLA Ops:
  0.0 139.7 %shard_map.73.refs_0_.refs_1_.refs_2_.refs_3_.refs_4_.refs_5_.refs_6_.refs_7_.refs_8_.refs_9_.refs_10_.refs_11_.refs_12_.refs_13_.refs_14_.refs_15_ = bf16[64,20,128,128]{3,2,1,0:T(8,128)(2,1)} custom-call(bf16[10,128,128]{2,1,0:T(8,128)(2,1)} %bitcast.4, bf16[10,128,128]{2,1,0:T(8,128)(2,1)} %bitcast.5), custom_call_target="tpu_custom_call" | custom-call | tf_op jit(solution)/shard_map/pallas_call | solution.py:142
  139.8 23.6 %shard_map.74.part_ref = bf16[4,64,32,128]{3,2,1,0:T(8,128)(2,1)} custom-call(s32[64]{0:T(128)} %bitcast.6, s32[64]{0:T(128)} %bitcast.7, s32[64]{0:T(128)} %owner.1, s32[64]{0:T(128)} %live.1, bf16[64,128,128]{2,1,0:T(8,128)(2,1)} %psi_ref.1, ...), custom_call_target="tpu_custom_call" | custom-call | flops 5368709120 | bytes 46137344 | tf_op jit(solution)/shard_map/pallas_call | solution.py:197
  163.4 31.0 %shard_map.75 = bf16[64,32,128]{2,1,0:T(8,128)(2,1)} custom-call(bf16[4,64,32,128]{3,2,1,0:T(8,128)(2,1)} %shard_map.74.part_ref), custom_call_target="tpu_custom_call" | custom-call | tf_op jit(solution)/shard_map/pallas_call | solution.py:267
  194.4 1.9 copy.9

commit v10 on v9

--- a/solution.py
+++ b/solution.py
@@ -11,13 +11,18 @@
 NY, NZ = 4, 8
 
 
+PIECES = (
+    ((0, 10, 1, "zy"), (10, 10, -1, "zy")),
+    ((0, 8, 1, "yz"), (8, 2, 1, "zy"), (10, 8, -1, "yz"), (18, 2, -1, "zy")),
+)
+
+
 def gather_kernel(l_ref, r_ref, g_ref, own_sem, recv, sent):
     e = lax.axis_index("env")
     y = lax.axis_index("y")
     z = lax.axis_index("z")
     c = lax.axis_index("core")
     half = l_ref.shape[0]
-    shards = (l_ref, r_ref)
 
     def dev(yy, zz, cc):
         return (e, lax.rem(yy + 2 * NY, NY), lax.rem(zz + 2 * NZ, NZ), cc)
@@ -32,106 +37,97 @@
     pl.semaphore_wait(barrier, len(peers))
 
     owns = []
-    for h in range(2):
-        cp = pltpu.make_async_copy(shards[h], g_ref.at[slot(y, z, c), pl.ds(h * half, half)], own_sem.at[h])
+    for h, src in enumerate((l_ref, r_ref)):
+        cp = pltpu.make_async_copy(src, g_ref.at[slot(y, z, c), pl.ds(h * half, half)], own_sem.at[h])
         cp.start()
         owns.append(cp)
 
-    def role(cc, first, second):
-        fsize, fstep = first
-        ssize, sstep = second
-        fplus, fminus = fsize // 2, fsize - 1 - fsize // 2
-        splus, sminus = ssize // 2, ssize - 1 - ssize // 2
+    def own_part(lo, n):
+        if lo < half:
+            return l_ref.at[pl.ds(lo, n)]
+        return r_ref.at[pl.ds(lo - half, n)]
+
+    zstep = lambda d: (0, d)
+    ystep = lambda d: (d, 0)
+    rings = {"z": (NZ, zstep), "y": (NY, ystep)}
+
+    def role(cc):
         sends = []
         partner = dev(y, z, 1 - cc)
-
-        def where(a, b, h):
-            sign = 1 - 2 * h
-            fy, fz = fstep(sign * a)
-            sy, sz = sstep(sign * b)
-            return y - fy - sy, z - fz - sz
-
-        def part(ref, h):
-            return ref.at[pl.ds(h * half, half)]
-
-        def item(a, b, h):
-            oy, oz = where(a, b, h)
-            return slot(oy, oz, cc)
-
-        def near(h, ring, d):
-            sign = 1 - 2 * h
-            dy, dz = ring(sign * d)
-            return dev(y + dy, z + dz, cc)
-
-        def send(src, a, b, h, target, kind):
-            s = item(a, b, h)
-            cp = pltpu.make_async_remote_copy(
-                src_ref=src, dst_ref=part(g_ref.at[s], h), send_sem=sent.at[s, h, kind],
-                recv_sem=recv.at[s, h], device_id=target, device_id_type=MESH)
-            cp.start()
-            sends.append(cp)
-
-        def wait_in(s, h):
-            cp = pltpu.make_async_remote_copy(
-                src_ref=part(g_ref.at[s], h), dst_ref=part(g_ref.at[s], h), send_sem=sent.at[s, h, 0],
-                recv_sem=recv.at[s, h], device_id=partner, device_id_type=MESH)
-            cp.wait_recv()
-
-        def held(a, b, h):
-            return part(g_ref.at[item(a, b, h)], h)
-
-        def spread(src, a, b, h):
-            if b == 0:
-                send(src, a, 0, h, near(h, sstep, 1), 2)
-                send(src, a, 0, h, near(h, sstep, -1), 3)
-            elif 0 < b < splus:
-                send(src, a, b, h, near(h, sstep, 1), 2)
-            elif 0 < -b < sminus:
-                send(src, a, b, h, near(h, sstep, -1), 3)
-            send(src, a, b, h, partner, 4)
-
-        for h in range(2):
-            send(shards[h], 0, 0, h, near(h, fstep, 1), 0)
-            send(shards[h], 0, 0, h, near(h, fstep, -1), 1)
-        for h in range(2):
-            spread(shards[h], 0, 0, h)
-        for step in range(1, max(fplus, fminus) + 1):
-            for a in (step, -step):
-                if (a > 0 and a > fplus) or (a < 0 and -a > fminus):
-                    continue
-                for h in range(2):
-                    wait_in(item(a, 0, h), h)
-                    if 0 < a < fplus:
-                        send(held(a, 0, h), a, 0, h, near(h, fstep, 1), 0)
-                    if 0 < -a < fminus:
-                        send(held(a, 0, h), a, 0, h, near(h, fstep, -1), 1)
-                    spread(held(a, 0, h), a, 0, h)
-        row = list(range(-fminus, fplus + 1))
-        for step in range(1, max(splus, sminus) + 1):
-            for b in (step, -step):
-                if (b > 0 and b > splus) or (b < 0 and -b > sminus):
-                    continue
-                for a in row:
-                    for h in range(2):
-                        wait_in(item(a, b, h), h)
-                        spread(held(a, b, h), a, b, h)
-        for yy in range(NY):
-            for zz in range(NZ):
-                for h in range(2):
-                    wait_in((yy * NZ + zz) * 2 + (1 - cc), h)
+        levels = {}
+
+        for pi, (lo, n, sign, order) in enumerate(PIECES[cc]):
+            fsize, fstep = rings[order[0]]
+            ssize, sstep = rings[order[1]]
+            fplus, fminus = fsize // 2, fsize - 1 - fsize // 2
+            splus, sminus = ssize // 2, ssize - 1 - ssize // 2
+
+            def item(a, b, fstep=fstep, sstep=sstep, sign=sign):
+                fy, fz = fstep(sign * a)
+                sy, sz = sstep(sign * b)
+                return slot(y - fy - sy, z - fz - sz, cc)
+
+            def near(ring, d, sign=sign):
+                dy, dz = ring(sign * d)
+                return dev(y + dy, z + dz, cc)
+
+            def send(src, a, b, target, kind, pi=pi, lo=lo, n=n, item=item):
+                s = item(a, b)
+                cp = pltpu.make_async_remote_copy(
+                    src_ref=src, dst_ref=g_ref.at[s, pl.ds(lo, n)], send_sem=sent.at[s, pi, kind],
+                    recv_sem=recv.at[s, pi], device_id=target, device_id_type=MESH)
+                cp.start()
+                sends.append(cp)
+
+            def handle(a, b, wait, pi=pi, lo=lo, n=n, item=item, near=near, send=send,
+                       fstep=fstep, sstep=sstep, fplus=fplus, fminus=fminus, splus=splus, sminus=sminus):
+                if wait:
+                    s = item(a, b)
+                    pltpu.make_async_remote_copy(
+                        src_ref=g_ref.at[s, pl.ds(lo, n)], dst_ref=g_ref.at[s, pl.ds(lo, n)],
+                        send_sem=sent.at[s, pi, 0], recv_sem=recv.at[s, pi], device_id=partner,
+                        device_id_type=MESH).wait_recv()
+                    src = g_ref.at[s, pl.ds(lo, n)]
+                else:
+                    src = own_part(lo, n)
+                if b == 0:
+                    if a == 0 or 0 < a < fplus:
+                        send(src, a, 0, near(fstep, 1), 0)
+                    if a == 0 or 0 < -a < fminus:
+                        send(src, a, 0, near(fstep, -1), 1)
+                    send(src, a, 0, near(sstep, 1), 2)
+                    send(src, a, 0, near(sstep, -1), 3)
+                elif 0 < b < splus:
+                    send(src, a, b, near(sstep, 1), 2)
+                elif 0 < -b < sminus:
+                    send(src, a, b, near(sstep, -1), 3)
+                send(src, a, b, partner, 4)
+
+            for a in range(-fminus, fplus + 1):
+                for b in range(-sminus, splus + 1):
+                    levels.setdefault(abs(a) + abs(b), []).append((handle, a, b))
+
+        for level in sorted(levels):
+            for handle, a, b in levels[level]:
+                handle(a, b, level > 0)
+        for pi, (lo, n, sign, order) in enumerate(PIECES[1 - cc]):
+            for yy in range(NY):
+                for zz in range(NZ):
+                    s = (yy * NZ + zz) * 2 + (1 - cc)
+                    pltpu.make_async_remote_copy(
+                        src_ref=g_ref.at[s, pl.ds(lo, n)], dst_ref=g_ref.at[s, pl.ds(lo, n)],
+                        send_sem=sent.at[s, pi, 0], recv_sem=recv.at[s, pi], device_id=partner,
+                        device_id_type=MESH).wait_recv()
         for cp in sends:
             cp.wait_send()
 
-    zstep = lambda d: (0, d)
-    ystep = lambda d: (d, 0)
-
     @pl.when(c == 0)
     def _():
-        role(0, (NZ, zstep), (NY, ystep))
+        role(0)
 
     @pl.when(c == 1)
     def _():
-        role(1, (NY, ystep), (NZ, zstep))
+        role(1)
 
     for cp in owns:
         cp.wait()
@@ -146,8 +142,8 @@
         out_specs=pl.BlockSpec(memory_space=pl.ANY),
         scratch_shapes=[
             pltpu.SemaphoreType.DMA((2,)),
-            pltpu.SemaphoreType.DMA((NY * NZ * 2, 2)),
-            pltpu.SemaphoreType.DMA((NY * NZ * 2, 2, 5)),
+            pltpu.SemaphoreType.DMA((NY * NZ * 2, 4)),
+            pltpu.SemaphoreType.DMA((NY * NZ * 2, 4, 5)),
         ],
         compiler_params=pltpu.CompilerParams(collective_id=0, has_side_effects=True),
     )(left, right)

time: 196 us -> 191 us (0.974)
  the two profiles are of different devices: /device:TPU:16 before, /device:TPU:1 now
where the time goes in v10:
time: 191 us
  Pallas kernels  189 us (99%)
    pallas_call x1, Pallas kernels, gather_env(): pl.pallas_call(gather_kernel, out_shape=jax.ShapeDtypeStruct(shape, left....  138 us
    pallas_call x1, Pallas kernels, exchange(): pl.pallas_call(exchange_kernel, out_shape=jax.ShapeDtypeStruct((count, sh...  29.5 us
    pallas_call x1, Pallas kernels, apply_blocks(): pl.pallas_call(block_kernel, grid_spec=grid_spec, out_shape=jax.ShapeDtyp...  22 us

profile of v10, /device:TPU:1, one launch (start us, length us, event | category | flops | bytes accessed | tf_op | source)
XLA Modules:
  0.0 191.1 jit_solution(6873849876031834979)
XLA Ops:
  0.0 137.6 %shard_map.73.refs_0_.refs_1_.refs_2_.refs_3_.refs_4_.refs_5_.refs_6_.refs_7_.refs_8_.refs_9_.refs_10_.refs_11_.refs_12_.refs_13_.refs_14_.refs_15_ = bf16[64,20,128,128]{3,2,1,0:T(8,128)(2,1)} custom-call(bf16[10,128,128]{2,1,0:T(8,128)(2,1)} %bitcast.4, bf16[10,128,128]{2,1,0:T(8,128)(2,1)} %bitcast.5), custom_call_target="tpu_custom_call" | custom-call | tf_op jit(solution)/shard_map/pallas_call | solution.py:138
  137.6 22.0 %shard_map.74.part_ref = bf16[4,64,32,128]{3,2,1,0:T(8,128)(2,1)} custom-call(s32[64]{0:T(128)} %bitcast.6, s32[64]{0:T(128)} %bitcast.7, s32[64]{0:T(128)} %owner.1, s32[64]{0:T(128)} %live.1, bf16[64,128,128]{2,1,0:T(8,128)(2,1)} %psi_ref.1, ...), custom_call_target="tpu_custom_call" | custom-call | flops 5368709120 | bytes 46137344 | tf_op jit(solution)/shard_map/pallas_call | solution.py:193
  159.7 29.5 %shard_map.75 = bf16[64,32,128]{2,1,0:T(8,128)(2,1)} custom-call(bf16[4,64,32,128]{3,2,1,0:T(8,128)(2,1)} %shard_map.74.part_ref), custom_call_target="tpu_custom_call" | custom-call | tf_op jit(solution)/shard_map/pallas_call | solution.py:263
  189.2 1.9 copy.9

commit v11 on v10

--- a/solution.py
+++ b/solution.py
@@ -248,21 +248,14 @@
     for cp in sends + [fwd_up, fwd_down]:
         cp.wait_send()
 
-    def body(j, carry):
-        total = got[0, j].astype(jnp.float32)
-        for s in range(1, nenv):
-            total = total + got[s, j].astype(jnp.float32)
-        out_ref[j] = total.astype(out_ref.dtype)
-        return carry
-
-    lax.fori_loop(0, count, body, 0)
+    out_ref[...] = got[...]
 
 
 def exchange(part):
     nenv, count, share, width = part.shape
     return pl.pallas_call(
         exchange_kernel,
-        out_shape=jax.ShapeDtypeStruct((count, share, width), part.dtype),
+        out_shape=jax.ShapeDtypeStruct((nenv, count, share, width), part.dtype),
         in_specs=[pl.BlockSpec(memory_space=pl.ANY)],
         out_specs=pl.BlockSpec(memory_space=pltpu.VMEM),
         scratch_shapes=[
@@ -284,7 +277,8 @@
     rsec = right_sector[:, 0]
     both = gather_env(left_env[:, 0], right_env[:, 0])
     part = apply_blocks(psi, both, lsec, rsec, sector_owner, sector_rows, nenv)
-    return exchange(part)
+    got = exchange(part)
+    return jnp.sum(got.astype(jnp.float32), axis=0).astype(jnp.bfloat16)
 
 
 def solution(mesh):

time: 191 us -> 195 us (1.021)
  Pallas kernels: 189 us -> 192 us
  other arithmetic: 0 us -> 2.85 us
    reduce_sum x0 -> x1, other arithmetic: none -> 2.85 us  [on_device(): return jnp.sum(got.astype(jnp.float32), axis=0).astype(jnp.bfloat16)]
where the time goes in v11:
time: 195 us
  Pallas kernels  192 us (98%)
  other arithmetic  2.85 us (1%)
    pallas_call x1, Pallas kernels, gather_env(): pl.pallas_call(gather_kernel, out_shape=jax.ShapeDtypeStruct(shape, left....  138 us
    pallas_call x1, Pallas kernels, exchange(): pl.pallas_call(exchange_kernel, out_shape=jax.ShapeDtypeStruct((nenv, cou...  30.4 us
    pallas_call x1, Pallas kernels, apply_blocks(): pl.pallas_call(block_kernel, grid_spec=grid_spec, out_shape=jax.ShapeDtyp...  23.6 us

profile of v11, /device:TPU:1, one launch (start us, length us, event | category | flops | bytes accessed | tf_op | source)
XLA Modules:
  0.0 194.5 jit_solution(7292262674392107569)
XLA Ops:
  0.0 137.6 %shard_map.73.refs_0_.refs_1_.refs_2_.refs_3_.refs_4_.refs_5_.refs_6_.refs_7_.refs_8_.refs_9_.refs_10_.refs_11_.refs_12_.refs_13_.refs_14_.refs_15_ = bf16[64,20,128,128]{3,2,1,0:T(8,128)(2,1)} custom-call(bf16[10,128,128]{2,1,0:T(8,128)(2,1)} %bitcast.4, bf16[10,128,128]{2,1,0:T(8,128)(2,1)} %bitcast.5), custom_call_target="tpu_custom_call" | custom-call | tf_op jit(solution)/shard_map/pallas_call | solution.py:138
  137.6 23.6 %shard_map.74.part_ref = bf16[4,64,32,128]{3,2,1,0:T(8,128)(2,1)} custom-call(s32[64]{0:T(128)} %bitcast.6, s32[64]{0:T(128)} %bitcast.7, s32[64]{0:T(128)} %owner.1, s32[64]{0:T(128)} %live.1, bf16[64,128,128]{2,1,0:T(8,128)(2,1)} %psi_ref.1, ...), custom_call_target="tpu_custom_call" | custom-call | flops 5368709120 | bytes 46137344 | tf_op jit(solution)/shard_map/pallas_call | solution.py:193
  161.2 30.4 %shard_map.75 = bf16[4,64,32,128]{3,2,1,0:T(8,128)(2,1)} custom-call(bf16[4,64,32,128]{3,2,1,0:T(8,128)(2,1)} %shard_map.74.part_ref), custom_call_target="tpu_custom_call" | custom-call | tf_op jit(solution)/shard_map/pallas_call | solution.py:256
  191.7 2.9 %reduce_sum.12 = bf16[64,32,128]{2,1,0:T(8,128)(2,1)} reduce(bf16[4,64,32,128]{3,2,1,0:T(8,128)(2,1)} %shard_map.75, bf16[]{:T(256)} %constant.2.clone.1), dimensions={0}, to_apply=%region_0.0 | reduce | flops 786432 | bytes 2621442 | tf_op jit(solution)/shard_map/reduce_sum | solution.py:281

commit v12 on v10

--- a/solution.py
+++ b/solution.py
@@ -172,7 +172,7 @@
             out_ref[r, j] = part[r * share:(r + 1) * share]
 
 
-def apply_blocks(psi, both, lsec, rsec, owner, live, nenv, group=8):
+def apply_blocks(psi, both, lsec, rsec, owner, live, nenv, group=16):
     count, width, _ = psi.shape
     share = width // nenv
     chans = both.shape[1] // 2

time: 191 us -> 195 us (1.021)
  Pallas kernels: 189 us -> 193 us
    pallas_call x1, Pallas kernels: 22 us -> 25.7 us  [apply_blocks(): pl.pallas_call(block_kernel, grid_spec=grid_spec, out_shape=jax.ShapeDtyp...]
where the time goes in v12:
time: 195 us
  Pallas kernels  193 us (99%)
    pallas_call x1, Pallas kernels, gather_env(): pl.pallas_call(gather_kernel, out_shape=jax.ShapeDtypeStruct(shape, left....  138 us
    pallas_call x1, Pallas kernels, exchange(): pl.pallas_call(exchange_kernel, out_shape=jax.ShapeDtypeStruct((count, sh...  30.1 us
    pallas_call x1, Pallas kernels, apply_blocks(): pl.pallas_call(block_kernel, grid_spec=grid_spec, out_shape=jax.ShapeDtyp...  25.7 us

profile of v12, /device:TPU:1, one launch (start us, length us, event | category | flops | bytes accessed | tf_op | source)
XLA Modules:
  0.0 195.3 jit_solution(274818498057710824)
XLA Ops:
  0.0 137.6 %shard_map.73.refs_0_.refs_1_.refs_2_.refs_3_.refs_4_.refs_5_.refs_6_.refs_7_.refs_8_.refs_9_.refs_10_.refs_11_.refs_12_.refs_13_.refs_14_.refs_15_.refs_16_.refs_17_.refs_18_.refs_19_.refs_20_.refs_21_.refs_22_.refs_23_.refs_24_.refs_25_.refs_26_.refs_27_.refs_28_.refs_29_.refs_30_.refs_31_ = bf16[64,20,128,128]{3,2,1,0:T(8,128)(2,1)} custom-call(bf16[10,128,128]{2,1,0:T(8,128)(2,1)} %bitcast.4, ...), custom_call_target="tpu_custom_call" | custom-call | tf_op jit(solution)/shard_map/pallas_call | solution.py:138
  137.6 25.7 %shard_map.74.part_ref = bf16[4,64,32,128]{3,2,1,0:T(8,128)(2,1)} custom-call(s32[64]{0:T(128)} %bitcast.6, s32[64]{0:T(128)} %bitcast.7, s32[64]{0:T(128)} %owner.1, s32[64]{0:T(128)} %live.1, bf16[64,128,128]{2,1,0:T(8,128)(2,1)} %psi_ref.1, ...), custom_call_target="tpu_custom_call" | custom-call | flops 5368709120 | bytes 46137344 | tf_op jit(solution)/shard_map/pallas_call | solution.py:193
  163.4 30.1 %shard_map.75 = bf16[64,32,128]{2,1,0:T(8,128)(2,1)} custom-call(bf16[4,64,32,128]{3,2,1,0:T(8,128)(2,1)} %shard_map.74.part_ref), custom_call_target="tpu_custom_call" | custom-call | tf_op jit(solution)/shard_map/pallas_call | solution.py:263
  193.5 1.9 copy.9

commit v13 on v10

--- a/solution.py
+++ b/solution.py
@@ -248,14 +248,17 @@
     for cp in sends + [fwd_up, fwd_down]:
         cp.wait_send()
 
+    step = 8
+
     def body(j, carry):
-        total = got[0, j].astype(jnp.float32)
+        blocks = pl.ds(pl.multiple_of(j * step, step), step)
+        total = got[0, blocks].astype(jnp.float32)
         for s in range(1, nenv):
-            total = total + got[s, j].astype(jnp.float32)
-        out_ref[j] = total.astype(out_ref.dtype)
+            total = total + got[s, blocks].astype(jnp.float32)
+        out_ref[blocks] = total.astype(out_ref.dtype)
         return carry
 
-    lax.fori_loop(0, count, body, 0)
+    lax.fori_loop(0, count // step, body, 0)
 
 
 def exchange(part):

time: 191 us -> 192 us (level)
  Pallas kernels: 189 us -> 191 us
where the time goes in v13:
time: 192 us; the launch traced here: 193 us
  Pallas kernels  191 us (99%)
    pallas_call x1, Pallas kernels, gather_env(): pl.pallas_call(gather_kernel, out_shape=jax.ShapeDtypeStruct(shape, left....  138 us
    pallas_call x1, Pallas kernels, exchange(): pl.pallas_call(exchange_kernel, out_shape=jax.ShapeDtypeStruct((count, sh...  29.9 us
    pallas_call x1, Pallas kernels, apply_blocks(): pl.pallas_call(block_kernel, grid_spec=grid_spec, out_shape=jax.ShapeDtyp...  23.2 us

profile of v13, /device:TPU:1, one launch (start us, length us, event | category | flops | bytes accessed | tf_op | source)
XLA Modules:
  0.0 192.5 jit_solution(4038726920942060768)
XLA Ops:
  0.0 137.6 %shard_map.73.refs_0_.refs_1_.refs_2_.refs_3_.refs_4_.refs_5_.refs_6_.refs_7_.refs_8_.refs_9_.refs_10_.refs_11_.refs_12_.refs_13_.refs_14_.refs_15_ = bf16[64,20,128,128]{3,2,1,0:T(8,128)(2,1)} custom-call(bf16[10,128,128]{2,1,0:T(8,128)(2,1)} %bitcast.4, bf16[10,128,128]{2,1,0:T(8,128)(2,1)} %bitcast.5), custom_call_target="tpu_custom_call" | custom-call | tf_op jit(solution)/shard_map/pallas_call | solution.py:138
  137.6 23.2 %shard_map.74.part_ref = bf16[4,64,32,128]{3,2,1,0:T(8,128)(2,1)} custom-call(s32[64]{0:T(128)} %bitcast.6, s32[64]{0:T(128)} %bitcast.7, s32[64]{0:T(128)} %owner.1, s32[64]{0:T(128)} %live.1, bf16[64,128,128]{2,1,0:T(8,128)(2,1)} %psi_ref.1, ...), custom_call_target="tpu_custom_call" | custom-call | flops 5368709120 | bytes 46137344 | tf_op jit(solution)/shard_map/pallas_call | solution.py:193
  160.8 29.9 %shard_map.75 = bf16[64,32,128]{2,1,0:T(8,128)(2,1)} custom-call(bf16[4,64,32,128]{3,2,1,0:T(8,128)(2,1)} %shard_map.74.part_ref), custom_call_target="tpu_custom_call" | custom-call | tf_op jit(solution)/shard_map/pallas_call | solution.py:266
  190.7 1.9 copy.9
